TPU v7x, 32 devices: a whole 2x2x4 slice. The times are simulated.
32 devices in a mesh: space: 8 (over y, x, core), chan: 4 (over z).
Axes of the slice: x: 2, y: 2, z: 4, core: 2. Of those that a mesh axis runs over, the one named last changes fastest.
Arguments:
- points: bfloat16 [256, 8, 16384], P('chan', 'space'), may hold values from -6 to 6
- point_cell: int32 [8, 16384], P('space'), may hold values from 0 to 4096, as said below
- conv_weight: bfloat16 [27, 256, 256], P(None, 'chan'), may hold values from -0.109375 to 0.109375
- conv_bias: bfloat16 [256], P('chan'), may hold values from -3 to 3
- neighbors: int32 [64, 27], P('space'), may hold values from -1 to 23, as said below
Outputs:
- voxel_out: bfloat16 [256, 32768], P('chan', 'space')
- point_out: bfloat16 [256, 8, 16384], P('chan', 'space')
Inputs may be any that keep to these rules, and one draw needn't show every extreme that they name: `point_cell`: in each aligned block of 2048 slots from one sender the live slots (cell below 4096) come first; in every draw some owner receives 2048 live slots from every sender. `neighbors`: entry 13 is the block's own slot 8 + b; blocks of one owner lie on a 4 x (4) grid of a strip, strips of owners d and d+1 adjacent.
All inputs are finite; a program needn't handle non-finite values.
Results may differ from a plain program's by a relative error of at most 0.01.
Values may be sent and summed in bfloat16 or wider, within the bound.
A program may use at most 128 MiB of HBM per device.

v0:
```python
import jax
import jax.numpy as jnp
import numpy as np
from jax import lax
from jax.sharding import PartitionSpec as P


def extended_2(cells, sides, width):
    for axis, dim in sides:
        count = lax.axis_size(axis)
        ends = count - 1
        head = lax.slice_in_dim(cells, 0, width, axis=dim)
        tail = lax.slice_in_dim(cells, cells.shape[dim] - width, cells.shape[dim], axis=dim)
        cells = jnp.concatenate(
            [
                lax.ppermute(tail, axis, [(i, (i + 1) % count) for i in range(ends)]),
                cells,
                lax.ppermute(head, axis, [((i + 1) % count, i) for i in range(ends)]),
            ],
            axis=dim,
        )
    return cells


def reach_tables(coord_x, coord_y, coord_z):

    def split_axis(values):
        moved = np.where(values < 0, -1, np.where(values > 7, 1, 0))
        return (moved, values - 8 * moved)

    move_x, inner_x = split_axis(coord_x)
    move_y, inner_y = split_axis(coord_y)
    move_z, inner_z = split_axis(coord_z)
    direction = 9 * (move_x + 1) + 3 * (move_y + 1) + (move_z + 1)
    inner = 64 * inner_x + 8 * inner_y + inner_z
    return (direction.astype(np.int32), inner.astype(np.int32))


def margin_tables():
    spots = np.arange(1000)
    return reach_tables(spots // 100 - 1, spots // 10 % 10 - 1, spots % 10 - 1)


def window_table():
    cells = np.arange(512)
    base = cells // 64 * 100 + cells // 8 % 8 * 10 + cells % 8
    shifts = np.arange(27)
    step = shifts // 9 * 100 + shifts // 3 % 3 * 10 + shifts % 3
    return (step[:, None] + base[None, :]).astype(np.int32)


def source_index(neighbors, direction, inner, spare):
    slots = jnp.take(neighbors, jnp.asarray(direction), axis=1)
    slots = jnp.where(slots < 0, spare, slots)
    return slots * 512 + jnp.asarray(inner)[None]


def pool_blocks(features, cell_ids, block_count):
    row_total = features.shape[1]
    step_rows = min(row_total, 2048)
    turns = row_total // step_rows
    targets = jnp.arange(block_count * 512, dtype=jnp.int32)
    width_here = features.shape[0]

    def accumulate(turn, carry):
        summed, tallies = carry
        rows = lax.dynamic_slice_in_dim(features, turn * step_rows, step_rows, 1)
        ids = lax.dynamic_slice_in_dim(cell_ids, turn * step_rows, step_rows, 0)
        onehot = (ids[:, None] == targets[None, :]).astype(jnp.bfloat16)
        summed = summed + jnp.dot(rows, onehot, preferred_element_type=jnp.float32)
        tallies = tallies + jnp.sum(onehot, axis=0, dtype=jnp.float32)
        return (summed, tallies)

    start = (
        jnp.zeros((width_here, block_count * 512), jnp.float32),
        jnp.zeros((block_count * 512,), jnp.float32),
    )
    summed, tallies = lax.fori_loop(0, turns, accumulate, start)
    voxels = (summed / jnp.maximum(tallies, 1.0)[None, :]).astype(jnp.bfloat16)
    return (voxels.reshape(width_here, block_count, 512), tallies)


def on_device(points, point_cell, conv_weight, conv_bias, neighbors):
    width_local = points.shape[0]
    owners = lax.axis_size("space")
    slot_total = points.shape[2]
    slot_cap = slot_total // owners
    block_count = neighbors.shape[0]
    arrived = lax.all_to_all(points, "space", split_axis=2, concat_axis=1, tiled=True)
    features = arrived.reshape(width_local, owners * slot_cap)
    cell_ids = point_cell[0]
    voxels, tallies = pool_blocks(features, cell_ids, block_count)
    active = jnp.where(tallies > 0.0, 1.0, 0.0).astype(jnp.float32)
    source = extended_2(voxels, (("space", 1),), block_count)
    source = jnp.concatenate([source, jnp.zeros((width_local, 1, 512), jnp.bfloat16)], 1)
    flat_source = source.reshape(width_local, (3 * block_count + 1) * 512)
    spare = 3 * block_count
    weight_all, bias_all = (
        lax.all_gather(conv_weight, "chan", axis=1, tiled=True),
        lax.all_gather(conv_bias, "chan", axis=0, tiled=True),
    )
    groups = lax.axis_size("chan")
    share = block_count // groups
    margin_dir, margin_inner = margin_tables()
    margin_index = source_index(neighbors, margin_dir, margin_inner, spare).reshape(
        block_count * 1000
    )
    margins = jnp.take(flat_source, margin_index, axis=1).reshape(width_local, block_count, 1000)
    spread = lax.all_to_all(margins, "chan", split_axis=1, concat_axis=0, tiled=True)
    width_all = spread.shape[0]
    flat_spread = spread.reshape(width_all, share * 1000)
    window = jnp.asarray(window_table())
    block_base = (jnp.arange(share, dtype=jnp.int32) * 1000)[None, :, None]
    column_index = (block_base + window[:, None, :]).reshape(27, share * 512)
    stacked = jnp.take(flat_spread, column_index, axis=1)
    total = jnp.zeros((width_all, share * 512), jnp.float32)
    for group in range(groups):
        low = group * width_local
        partial_sum = jnp.einsum(
            "ion,oic->cn",
            stacked[low : low + width_local],
            weight_all[:, low : low + width_local, :],
            preferred_element_type=jnp.float32,
        ).astype(jnp.bfloat16)
        partial_sum = lax.optimization_barrier(partial_sum)
        total = total + partial_sum.astype(jnp.float32)
    mine = lax.dynamic_slice_in_dim(active, lax.axis_index("chan") * (share * 512), share * 512, 0)
    finished = (
        jnp.maximum(total + bias_all.astype(jnp.float32)[:, None], 0.0) * mine[None, :]
    ).astype(jnp.bfloat16)
    voxel_out = lax.all_to_all(finished, "chan", split_axis=0, concat_axis=1, tiled=True)
    extended = jnp.concatenate([voxel_out, jnp.zeros((width_local, 1), jnp.bfloat16)], 1)
    picked = jnp.take(extended, cell_ids, axis=1).reshape(width_local, owners, slot_cap)
    returned = lax.all_to_all(picked, "space", split_axis=1, concat_axis=2, tiled=True)
    point_out = (points.astype(jnp.float32) + returned.astype(jnp.float32)).astype(jnp.bfloat16)
    return (voxel_out, point_out)


def solution(mesh):
    return jax.shard_map(
        on_device,
        mesh=mesh,
        in_specs=(
            P("chan", "space", None),
            P("space", None),
            P(None, "chan", None),
            P("chan"),
            P("space", None),
        ),
        out_specs=(P("chan", "space"), P("chan", "space", None)),
        check_vma=False,
    )
```

profile of v0, /device:TPU:11, one launch (start us, length us, event | category | flops | bytes accessed | tf_op | source)
XLA Modules:
  0.0 656.9 jit_solution(425877067838428987)
XLA Ops:
  7.2 17.2 %copy.80 = bf16[64,1,16384]{0,1,2:T(2,128)(2,1)} copy(bf16[64,1,16384]{2,0,1:T(8,128)(2,1)} %param.10) | data formatting | bytes 4194304 | tf_op args[0]
  24.9 90.8 %reduce.6 = bf16[16384,64]{1,0:T(8,128)(2,1)} reduce(bf16[16384,1,64]{2,1,0:T(2,128)(2,1)} %bitcast.73, bf16[]{:T(256)} %broadcast.224), dimensions={1}, to_apply=%bitcast.69.reduce_sub_computation | reduce | bytes 4194306
  115.6 7.6 %reshape.286 = bf16[8,2,65536]{2,1,0:T(2,128)(2,1)} reshape(bf16[16384,64]{1,0:T(8,128)(2,1)} %reduce.6) | data formatting | bytes 4194304
  123.2 4.7 all-to-all-start
  128.8 2.9 gather_fusion
  132.2 20.8 %all-to-all-done = bf16[8,2,65536]{2,1,0:T(2,128)(2,1)S(1)} async-done(((bf16[8,2,65536]{2,1,0:T(2,128)(2,1)}), bf16[8,2,65536]{2,1,0:T(2,128)(2,1)S(1)}, u32[]{:S(2)}, u32[]{:S(2)}) %all-to-all-start) | async-done | bytes 2097184 | tf_op jit(solution)/shard_map/all_to_all | solution.py:89
  153.0 5.9 reshape.287
  158.8 15.5 %copy.81 = bf16[64,1,16384]{2,0,1:T(8,128)(2,1)S(1)} copy(bf16[64,1,16384]{0,1,2:T(2,128)(2,1)} %bitcast.74) | data formatting | bytes 4194304 | tf_op jit(solution)/shard_map/all_to_all | solution.py:89
  174.3 115.7 %while.16 = (s32[]{:T(128)}, f32[64,4096]{1,0:T(8,128)}, f32[4096]{0:T(1024)S(1)}, bf16[64,16384]{1,0:T(8,128)(2,1)S(1)}, s32[16384]{0:T(1024)S(1)}, /*index=5*/s32[]{:T(128)}, s32[]{:T(128)}, s32[]{:T(128)}, s32[]{:T(128)}) while((s32[]{:T(128)}, f32[64,4096]{1,0:T(8,128)}, f32[4096]{0:T(1024)S(1)}, ...), condition=%wide.region_2.0_spmd.clone, body=%wide.region_0.0_spmd.clone.sunk | while | flops 1116213248 | bytes 2457758 | solution.py:78
  174.6 8.0 %fusion.65 = f32[64,4096]{1,0:T(8,128)} fusion(s32[2048]{0:T(1024)S(1)} %dynamic_slice.29, f32[64,4096]{1,0:T(8,128)} %get-tuple-element.202, pred[]{:T(512)S(6)} %compare.4, bf16[64,16384]{1,0:T(8,128)(2,1)S(1)} %get-tuple-element.213, s32[]{:T(128)S(6)} %select_n.172), kind=kOutput, calls=%fused_computation.10.clone.1 | convolution fusion | flops 1082654720 | bytes 2367493 | tf_op jit(solution)/shard_map/while/body/eval_jaxpr/dot_general | solution.py:70
  182.6 5.3 convert_reduce_fusion.2
  187.9 9.2 %fusion.65 = f32[64,4096]{1,0:T(8,128)} fusion(s32[2048]{0:T(1024)S(1)} %dynamic_slice.29, f32[64,4096]{1,0:T(8,128)} %get-tuple-element.202, pred[]{:T(512)S(6)} %compare.4, bf16[64,16384]{1,0:T(8,128)(2,1)S(1)} %get-tuple-element.213, s32[]{:T(128)S(6)} %select_n.172), kind=kOutput, calls=%fused_computation.10.clone.1 | convolution fusion | flops 1082654720 | bytes 2367493 | tf_op jit(solution)/shard_map/while/body/eval_jaxpr/dot_general | solution.py:70
  197.1 5.3 convert_reduce_fusion.2
  202.5 9.2 %fusion.65 = f32[64,4096]{1,0:T(8,128)} fusion(s32[2048]{0:T(1024)S(1)} %dynamic_slice.29, f32[64,4096]{1,0:T(8,128)} %get-tuple-element.202, pred[]{:T(512)S(6)} %compare.4, bf16[64,16384]{1,0:T(8,128)(2,1)S(1)} %get-tuple-element.213, s32[]{:T(128)S(6)} %select_n.172), kind=kOutput, calls=%fused_computation.10.clone.1 | convolution fusion | flops 1082654720 | bytes 2367493 | tf_op jit(solution)/shard_map/while/body/eval_jaxpr/dot_general | solution.py:70
  211.7 5.3 convert_reduce_fusion.2
  217.0 9.2 %fusion.65 = f32[64,4096]{1,0:T(8,128)} fusion(s32[2048]{0:T(1024)S(1)} %dynamic_slice.29, f32[64,4096]{1,0:T(8,128)} %get-tuple-element.202, pred[]{:T(512)S(6)} %compare.4, bf16[64,16384]{1,0:T(8,128)(2,1)S(1)} %get-tuple-element.213, s32[]{:T(128)S(6)} %select_n.172), kind=kOutput, calls=%fused_computation.10.clone.1 | convolution fusion | flops 1082654720 | bytes 2367493 | tf_op jit(solution)/shard_map/while/body/eval_jaxpr/dot_general | solution.py:70
  226.3 5.3 convert_reduce_fusion.2
  231.6 9.2 %fusion.65 = f32[64,4096]{1,0:T(8,128)} fusion(s32[2048]{0:T(1024)S(1)} %dynamic_slice.29, f32[64,4096]{1,0:T(8,128)} %get-tuple-element.202, pred[]{:T(512)S(6)} %compare.4, bf16[64,16384]{1,0:T(8,128)(2,1)S(1)} %get-tuple-element.213, s32[]{:T(128)S(6)} %select_n.172), kind=kOutput, calls=%fused_computation.10.clone.1 | convolution fusion | flops 1082654720 | bytes 2367493 | tf_op jit(solution)/shard_map/while/body/eval_jaxpr/dot_general | solution.py:70
  240.8 5.3 convert_reduce_fusion.2
  246.2 9.2 %fusion.65 = f32[64,4096]{1,0:T(8,128)} fusion(s32[2048]{0:T(1024)S(1)} %dynamic_slice.29, f32[64,4096]{1,0:T(8,128)} %get-tuple-element.202, pred[]{:T(512)S(6)} %compare.4, bf16[64,16384]{1,0:T(8,128)(2,1)S(1)} %get-tuple-element.213, s32[]{:T(128)S(6)} %select_n.172), kind=kOutput, calls=%fused_computation.10.clone.1 | convolution fusion | flops 1082654720 | bytes 2367493 | tf_op jit(solution)/shard_map/while/body/eval_jaxpr/dot_general | solution.py:70
  255.4 5.3 convert_reduce_fusion.2
  260.7 9.2 %fusion.65 = f32[64,4096]{1,0:T(8,128)} fusion(s32[2048]{0:T(1024)S(1)} %dynamic_slice.29, f32[64,4096]{1,0:T(8,128)} %get-tuple-element.202, pred[]{:T(512)S(6)} %compare.4, bf16[64,16384]{1,0:T(8,128)(2,1)S(1)} %get-tuple-element.213, s32[]{:T(128)S(6)} %select_n.172), kind=kOutput, calls=%fused_computation.10.clone.1 | convolution fusion | flops 1082654720 | bytes 2367493 | tf_op jit(solution)/shard_map/while/body/eval_jaxpr/dot_general | solution.py:70
  270.0 5.3 convert_reduce_fusion.2
  275.3 9.2 %fusion.65 = f32[64,4096]{1,0:T(8,128)} fusion(s32[2048]{0:T(1024)S(1)} %dynamic_slice.29, f32[64,4096]{1,0:T(8,128)} %get-tuple-element.202, pred[]{:T(512)S(6)} %compare.4, bf16[64,16384]{1,0:T(8,128)(2,1)S(1)} %get-tuple-element.213, s32[]{:T(128)S(6)} %select_n.172), kind=kOutput, calls=%fused_computation.10.clone.1 | convolution fusion | flops 1082654720 | bytes 2367493 | tf_op jit(solution)/shard_map/while/body/eval_jaxpr/dot_general | solution.py:70
  284.5 5.3 convert_reduce_fusion.2
  291.5 3.5 collective-permute-start
  297.6 6.4 collective-permute-done
  304.0 3.5 collective-permute-done.1
  309.6 3.9 copy.82
  313.5 17.3 %gather_fusion.1 = bf16[8000,64]{1,0:T(8,128)(2,1)} fusion(bf16[64,12800]{0,1:T(8,128)(2,1)S(1)} %bitcast.72, s32[8192]{0:T(1024)S(1)} %pad_clamp_fusion), kind=kCustom, calls=%fused_computation.1 | custom fusion | bytes 2080000 | tf_op jit(solution)/shard_map/jit(_take)/gather | solution.py:108
  333.9 4.8 all-to-all-start.1
  340.5 23.6 %all-reduce.1 = bf16[256]{0:T(256)(128)(2,1)S(1)} all-reduce(bf16[256]{0:T(256)(128)(2,1)S(1)} %dynamic-update-slice), channel_id=1, replica_groups=mesh['space'=8,'chan'=4] {'chan'}, use_global_device_ids=true, to_apply=%add.1 | all-reduce | flops 256 | bytes 1024
  366.6 3.8 copy.94
  371.7 109.4 %gather_fusion.2 = bf16[27648,256]{1,0:T(8,128)(2,1)} fusion(bf16[256,2000]{0,1:T(8,128)(2,1)S(1)} %reshape.274, s32[27648]{0:T(1024)S(1)} %broadcast_clamp_fusion), kind=kCustom, calls=%fused_computation.2 | custom fusion | bytes 28422144 | tf_op jit(solution)/shard_map/jit(_take)/gather | solution.py:115
  481.1 18.7 %copy.88 = bf16[27,1024,256]{1,2,0:T(8,128)(2,1)} copy(bf16[27,1024,256]{2,1,0:T(8,128)(2,1)} %bitcast.71) | data formatting | bytes 28311552 | tf_op jit(solution)/shard_map/jit(_take)/gather | solution.py:115
  499.7 12.6 %select_bitcast_fusion = bf16[256,27,1024]{2,0,1:T(8,128)(2,1)} fusion(bf16[27,1024,256]{1,2,0:T(8,128)(2,1)} %copy.88, pred[27,1024]{1,0:T(8,128)(4,1)S(1)} %compare_and_fusion.1), kind=kLoop, calls=%fused_computation.14 | loop fusion | flops 7077888 | bytes 28339200 | tf_op jit(solution)/shard_map/jit(_take)/select_n | solution.py:115
  512.4 3.6 fusion.40
  515.9 2.8 copy-done
  525.0 4.2 all-to-all-start.2
  529.2 10.6 %all-to-all-done.2 = bf16[4,64,1024]{2,1,0:T(8,128)(2,1)S(1)} async-done(((bf16[4,64,1024]{2,1,0:T(8,128)(2,1)}), bf16[4,64,1024]{2,1,0:T(8,128)(2,1)S(1)}, u32[]{:S(2)}, u32[]{:S(2)}) %all-to-all-start.2) | async-done | bytes 524320 | tf_op jit(solution)/shard_map/all_to_all | solution.py:131
  540.5 57.8 %gather_fusion.3 = bf16[16384,64]{1,0:T(8,128)(2,1)} fusion(bf16[64,4097]{0,1:T(8,128)(2,1)S(1)} %concatenate.7, s32[16384]{0:T(1024)S(1)} %broadcast_clamp_fusion.1), kind=kCustom, calls=%fused_computation.3 | custom fusion | bytes 4259840 | tf_op jit(solution)/shard_map/jit(_take)/gather | solution.py:133
  598.3 4.8 copy.91
  603.0 3.1 broadcast_select_fusion
  606.2 5.0 all-to-all-start.3
  612.3 24.0 %all-to-all-done.3 = bf16[64,8,2048]{2,0,1:T(8,128)(2,1)} async-done(((bf16[64,8,2048]{2,0,1:T(8,128)(2,1)}), bf16[64,8,2048]{2,0,1:T(8,128)(2,1)}, u32[]{:S(2)}, u32[]{:S(2)}) %all-to-all-start.3) | async-done | bytes 2097184 | tf_op jit(solution)/shard_map/all_to_all | solution.py:134
  636.3 4.8 copy.92
  641.1 5.1 reshape.231
  646.2 3.9 add_convert_fusion
  (93 shorter events, 24.1 us)
Async XLA Ops:
  123.2 5.4 copy-start.6
  123.2 5.5 copy-start.7
  123.2 8.7 %copy-start.5 = (s32[1000]{0:T(1024)S(1)}, s32[1000]{0:T(1024)}, u32[]{:S(2)}) copy-start(s32[1000]{0:T(1024)} %constant.126.clone) | copy-start | bytes 12004
  123.2 8.9 %copy-start.3 = (s32[1,16384]{1,0:T(1,128)S(1)}, s32[1,16384]{1,0:T(1,128)}, u32[]{:S(2)}) copy-start(s32[1,16384]{1,0:T(1,128)} %param.11) | copy-start | bytes 196612
  123.2 29.7 %all-to-all-start = ((bf16[8,2,65536]{2,1,0:T(2,128)(2,1)}), bf16[8,2,65536]{2,1,0:T(2,128)(2,1)S(1)}, u32[]{:S(2)}, u32[]{:S(2)}) async-start(bf16[8,2,65536]{2,1,0:T(2,128)(2,1)} %reshape.286), calls=%async_computation | async-start | bytes 4194304 | tf_op jit(solution)/shard_map/all_to_all | solution.py:89
  127.9 384.5 %all-gather.2.cloned.1.call-start = ((), (), s32[]{:S(2)}) async-start(), calls=%async_computation.4 | async-start | bytes 4423680 | tf_op jit(solution)/shard_map/all_gather | solution.py:99
  291.5 12.5 %collective-permute-start = (bf16[64,8,512]{2,1,0:T(8,128)(2,1)S(1)}, bf16[64,8,512]{2,1,0:T(8,128)(2,1)S(1)}, u32[]{:S(2)}, u32[]{:S(2)}) collective-permute-start(bf16[64,8,512]{2,1,0:T(8,128)(2,1)S(1)} %bitcast.84), channel_id=1, source_target_pairs={{0,4},{4,8},{8,12},{12,16},{16,20},{20,24},{24,28},{1,5},{5,9},{9,... | collective-permute-start | bytes 1572872 | tf_op jit(solution)/shard_map/ppermute | solution.py:16
  295.0 12.5 %collective-permute-start.1 = (bf16[64,8,512]{2,1,0:T(8,128)(2,1)S(1)}, bf16[64,8,512]{2,1,0:T(8,128)(2,1)S(1)}, u32[]{:S(2)}, u32[]{:S(2)}) collective-permute-start(bf16[64,8,512]{2,1,0:T(8,128)(2,1)S(1)} %bitcast.85), channel_id=1, source_target_pairs={{4,0},{8,4},{12,8},{16,12},{20,16},{24,20},{28,24},{5,1},{9,5},{13... | collective-permute-start | bytes 1572872 | tf_op jit(solution)/shard_map/ppermute | solution.py:18
  330.8 7.9 %copy-start.4 = (s32[27,512]{1,0:T(8,128)S(1)}, s32[27,512]{1,0:T(8,128)}, u32[]{:S(2)}) copy-start(s32[27,512]{1,0:T(8,128)} %constant.127.clone) | copy-start | bytes 165892
  332.8 6.3 copy-start.10
  332.8 7.5 %copy-start.9 = (bf16[64]{0:T(256)(128)(2,1)S(1)}, bf16[64]{0:T(256)(128)(2,1)}, u32[]{:S(2)}) copy-start(bf16[64]{0:T(256)(128)(2,1)} %param.13) | copy-start | bytes 388
  333.9 31.7 %all-to-all-start.1 = ((bf16[64,8,1000]{2,0,1:T(8,128)(2,1)}), bf16[64,8,1000]{2,0,1:T(8,128)(2,1)S(1)}, u32[]{:S(2)}, u32[]{:S(2)}) async-start(bf16[64,8,1000]{2,0,1:T(8,128)(2,1)} %broadcast_select_fusion.1), calls=%async_computation.1 | async-start | bytes 2097152 | tf_op jit(solution)/shard_map/all_to_all | solution.py:109
  365.6 1.0 copy-start.2
  512.4 6.4 copy-start
  518.7 2.5 copy-start.8
  525.0 14.8 %all-to-all-start.2 = ((bf16[4,64,1024]{2,1,0:T(8,128)(2,1)}), bf16[4,64,1024]{2,1,0:T(8,128)(2,1)S(1)}, u32[]{:S(2)}, u32[]{:S(2)}) async-start(bf16[4,64,1024]{2,1,0:T(8,128)(2,1)} %bitcast.19), calls=%async_computation.2 | async-start | bytes 1048576 | tf_op jit(solution)/shard_map/all_to_all | solution.py:131
  606.2 30.2 %all-to-all-start.3 = ((bf16[64,8,2048]{2,0,1:T(8,128)(2,1)}), bf16[64,8,2048]{2,0,1:T(8,128)(2,1)}, u32[]{:S(2)}, u32[]{:S(2)}) async-start(bf16[64,8,2048]{2,0,1:T(8,128)(2,1)} %broadcast_select_fusion), calls=%async_computation.3 | async-start | bytes 4194304 | tf_op jit(solution)/shard_map/all_to_all | solution.py:134
  641.1 5.1 copy-start.1
Sparse Core Ops, SparseCore 0:
  130.3 68.1 all-gather.1
where the time goes:
time: 665 us; the launch traced here: 657 us
  local copies, waits for them, and re-layouts  288 us (43%)
  other arithmetic  159 us (24%)
  matrix products  81 us (12%)
  waiting for transfers between devices  66 us (10%)
  starting transfers between devices  24 us (4%)
  blocking collectives  23.6 us (4%)
  between operations  15.1 us (2%)
    gather x2, local copies, waits for them, and re-layouts, on_device(): stacked = jnp.take(flat_spread, column_index, axis=1)  128 us
    unnamed x4, other arithmetic  91.6 us
    dot_general x8, matrix products, accumulate(): summed = summed + jnp.dot(rows, onehot, preferred_element_type=jnp.float32)  72.6 us
    gather x2, local copies, waits for them, and re-layouts, on_device(): jnp.take(extended, cell_ids, axis=1).reshape(width_local, owners, slot_cap)  62.5 us
    reduce_sum x8, other arithmetic, accumulate(): tallies = tallies + jnp.sum(onehot, axis=0, dtype=jnp.float32)  42.2 us
    unnamed x37, local copies, waits for them, and re-layouts  37.8 us
    all_to_all x1, waiting for transfers between devices, on_device(): lax.all_to_all(picked, 'space', split_axis=1, concat_axis=2, tiled=True)  24 us
    unnamed x1, blocking collectives  23.6 us
  transfers between devices with their start and end apart: 7, of which 5 were waited for; matrix products, arithmetic and copies ran while one was open for 48% of the time, Pallas kernels for 0%

commit v1 on v0

v1 whole, which is shorter than its diff:
```python
import functools

import jax
import jax.numpy as jnp
from jax import lax
from jax.experimental import pallas as pl
from jax.experimental.pallas import tpu as pltpu
from jax.sharding import PartitionSpec as P

VMEM_LIMIT = 60 * 1024 * 1024
CELLS = 512
ROWS = 1008


def params():
    return pltpu.CompilerParams(vmem_limit_bytes=VMEM_LIMIT)


def split_kernel(x_ref, o_ref):
    o_ref[0] = x_ref[...]


def split_slots(points, owners, cap):
    width = points.shape[0]
    return pl.pallas_call(
        split_kernel,
        grid=(owners,),
        in_specs=[pl.BlockSpec((width, cap), lambda d: (0, d))],
        out_specs=pl.BlockSpec((1, width, cap), lambda d: (d, 0, 0)),
        out_shape=jax.ShapeDtypeStruct((owners, width, cap), jnp.bfloat16),
        compiler_params=params(),
    )(points)


def pool_kernel(groups, low_cells, x_ref, id_ref, count_ref, o_ref, acc_ref):
    turn = pl.program_id(0)
    width, rows = x_ref.shape[1], x_ref.shape[2]

    @pl.when(turn == 0)
    def _():
        acc_ref[...] = jnp.zeros_like(acc_ref)

    ids = id_ref[0]
    high = ids // low_cells
    low = ids % low_cells
    x = x_ref[0]
    zero = jnp.zeros_like(x)
    masked = jnp.concatenate(
        [jnp.where(jnp.broadcast_to(high, x.shape) == g, x, zero) for g in range(groups)], axis=0
    )
    spots = lax.broadcasted_iota(jnp.int32, (low_cells, rows), 0)
    onehot = jnp.where(spots == low, 1.0, 0.0).astype(jnp.bfloat16)
    acc_ref[...] += lax.dot_general(
        onehot, masked, (((1,), (1,)), ((), ())), preferred_element_type=jnp.float32
    )

    @pl.when(turn == pl.num_programs(0) - 1)
    def _():
        for g in range(groups):
            lanes = slice(g * width, (g + 1) * width)
            tally = jnp.maximum(count_ref[:, g : g + 1], 1.0)
            o_ref[:, lanes] = (acc_ref[:, lanes] / tally).astype(jnp.bfloat16)


def pool(arrived, ids, counts, groups):
    owners, width, cap = arrived.shape
    low_cells = counts.shape[0] // groups
    by_group = counts.reshape(groups, low_cells).T
    return pl.pallas_call(
        functools.partial(pool_kernel, groups, low_cells),
        grid=(owners,),
        in_specs=[
            pl.BlockSpec((1, width, cap), lambda s: (s, 0, 0)),
            pl.BlockSpec((1, 1, cap), lambda s: (s, 0, 0)),
            pl.BlockSpec((low_cells, groups), lambda s: (0, 0)),
        ],
        out_specs=pl.BlockSpec((low_cells, groups * width), lambda s: (0, 0)),
        out_shape=jax.ShapeDtypeStruct((low_cells, groups * width), jnp.bfloat16),
        scratch_shapes=[pltpu.VMEM((low_cells, groups * width), jnp.float32)],
        compiler_params=params(),
    )(arrived, ids.reshape(owners, 1, cap), by_group)


def margin_kernel(groups, share, nb_ref, left_ref, own_ref, right_ref, bias_ref, o_ref, v_ref, m_ref):
    blocks = groups * share
    width = bias_ref.shape[1]
    for a, ref in enumerate((left_ref, own_ref, right_ref)):
        for g in range(groups):
            for lb in range(share):
                part = ref[lb * CELLS : (lb + 1) * CELLS, g * width : (g + 1) * width]
                v_ref[a * blocks + g * share + lb] = part.astype(jnp.float32).reshape(64, 8, width)
    v_ref[3 * blocks] = jnp.zeros((64, 8, width), jnp.float32)
    bias = jnp.broadcast_to(bias_ref[...].astype(jnp.float32), (8, width))
    spans = (((0, 7),), tuple((t + 1, t) for t in range(8)), ((9, 0),))

    def one_block(b, carry):
        for dx in range(3):
            for dy in range(3):
                for dz in range(3):
                    slot = nb_ref[b, 9 * dx + 3 * dy + dz]
                    slot = jnp.where(slot < 0, 3 * blocks, slot)
                    for xd, xs in spans[dx]:
                        for yd, ys in spans[dy]:
                            row = 100 * xd + 10 * yd
                            if dz == 1:
                                m_ref[b, row + 1 : row + 9, :] = v_ref[slot, 8 * xs + ys]
                            else:
                                zd, zs = spans[dz][0]
                                m_ref[b, row + zd : row + zd + 1, :] = v_ref[slot, 8 * xs + ys, zs : zs + 1, :]
        m_ref[b, 1000:ROWS, :] = bias
        return carry

    lax.fori_loop(0, blocks, one_block, 0)
    for g in range(groups):
        for lb in range(share):
            o_ref[g, :, lb * width : (lb + 1) * width] = m_ref[g * share + lb].astype(jnp.bfloat16)


def build_margins(neighbors, left, own, right, bias, groups, share):
    width = bias.shape[1]
    blocks = groups * share
    vmem = pl.BlockSpec(memory_space=pltpu.VMEM)
    return pl.pallas_call(
        functools.partial(margin_kernel, groups, share),
        in_specs=[pl.BlockSpec(memory_space=pltpu.SMEM), vmem, vmem, vmem, vmem],
        out_specs=vmem,
        out_shape=jax.ShapeDtypeStruct((groups, ROWS, share * width), jnp.bfloat16),
        scratch_shapes=[
            pltpu.VMEM((3 * blocks + 1, 64, 8, width), jnp.float32),
            pltpu.VMEM((blocks, ROWS, width), jnp.float32),
        ],
        compiler_params=params(),
    )(neighbors, left, own, right, bias)


def conv_kernel(share, m_ref, w_ref, act_ref, o_ref, f_ref, q_ref):
    groups, _, width, outs = w_ref.shape
    wide = groups * width
    for lb in range(share):
        for g in range(groups):
            f_ref[lb, :, g * width : (g + 1) * width] = m_ref[g, :, lb * width : (lb + 1) * width].astype(jnp.float32)
    for k in range(3):
        for lb in range(share):
            for p in range(6):
                for y in range(10):
                    near = 100 * p + 10 * y + k
                    far = near + 400
                    q_ref[k, lb, p, y] = jnp.concatenate(
                        [f_ref[lb, near : near + 8, :], f_ref[lb, far : far + 8, :]], axis=0
                    ).astype(jnp.bfloat16)
    bias = f_ref[0, 1000:1001, :]
    for lb in range(share):
        total = None
        for k in range(3):
            windows, weights = [], []
            for i in range(3):
                for j in range(3):
                    windows.append(q_ref[k, lb, i : i + 4, j : j + 8].reshape(CELLS, wide))
                    for g in range(groups):
                        weights.append(w_ref[g, 9 * i + 3 * j + k])
            term = jnp.dot(
                jnp.concatenate(windows, axis=1),
                jnp.concatenate(weights, axis=0),
                preferred_element_type=jnp.float32,
            )
            total = term if total is None else total + term
        total = jnp.maximum(total + bias, 0.0).reshape(4, 8, 2, 8, outs)
        for h in range(2):
            half = total[:, :, h].reshape(256, outs).T
            seg = slice(lb * CELLS + h * 256, lb * CELLS + (h + 1) * 256)
            o_ref[:, seg] = (half * act_ref[:, seg]).astype(jnp.bfloat16)


def convolve(spread, weight_all, active, share):
    groups, _, width, outs = weight_all.shape
    vmem = pl.BlockSpec(memory_space=pltpu.VMEM)
    return pl.pallas_call(
        functools.partial(conv_kernel, share),
        in_specs=[vmem] * 3,
        out_specs=vmem,
        out_shape=jax.ShapeDtypeStruct((outs, share * CELLS), jnp.bfloat16),
        scratch_shapes=[
            pltpu.VMEM((share, ROWS, groups * width), jnp.float32),
            pltpu.VMEM((3, share, 6, 10, 16, groups * width), jnp.bfloat16),
        ],
        compiler_params=params(),
    )(spread, weight_all, active)


def pick_kernel(groups, v_ref, id_ref, o_ref, vox_ref):
    width, low_cells = v_ref.shape[0] // groups, v_ref.shape[1]
    rows = id_ref.shape[2]

    @pl.when(pl.program_id(0) == 0)
    def _():
        for g in range(groups):
            vox_ref[:, g * low_cells : (g + 1) * low_cells] = v_ref[g * width : (g + 1) * width, :]

    ids = id_ref[0]
    high = ids // low_cells
    low = ids % low_cells
    spots = lax.broadcasted_iota(jnp.int32, (low_cells, rows), 0)
    onehot = jnp.where(spots == low, 1.0, 0.0).astype(jnp.bfloat16)
    found = jnp.dot(v_ref[...], onehot, preferred_element_type=jnp.float32)
    total = jnp.zeros((width, rows), jnp.float32)
    for g in range(groups):
        total = jnp.where(jnp.broadcast_to(high, total.shape) == g, found[g * width : (g + 1) * width], total)
    o_ref[0] = total.astype(jnp.bfloat16)


def pick(parts, ids, owners, cap):
    groups, width, low_cells = parts.shape
    return pl.pallas_call(
        functools.partial(pick_kernel, groups),
        grid=(owners,),
        in_specs=[
            pl.BlockSpec((groups * width, low_cells), lambda s: (0, 0)),
            pl.BlockSpec((1, 1, cap), lambda s: (s, 0, 0)),
        ],
        out_specs=[
            pl.BlockSpec((1, width, cap), lambda s: (s, 0, 0)),
            pl.BlockSpec((width, groups * low_cells), lambda s: (0, 0)),
        ],
        out_shape=[
            jax.ShapeDtypeStruct((owners, width, cap), jnp.bfloat16),
            jax.ShapeDtypeStruct((width, groups * low_cells), jnp.bfloat16),
        ],
        compiler_params=params(),
    )(parts.reshape(groups * width, low_cells), ids.reshape(owners, 1, cap))


def add_kernel(p_ref, r_ref, o_ref):
    o_ref[...] = (p_ref[...].astype(jnp.float32) + r_ref[0].astype(jnp.float32)).astype(jnp.bfloat16)


def add_back(points, returned):
    owners, width, cap = returned.shape
    return pl.pallas_call(
        add_kernel,
        grid=(owners,),
        in_specs=[
            pl.BlockSpec((width, cap), lambda d: (0, d)),
            pl.BlockSpec((1, width, cap), lambda d: (d, 0, 0)),
        ],
        out_specs=pl.BlockSpec((width, cap), lambda d: (0, d)),
        out_shape=jax.ShapeDtypeStruct(points.shape, jnp.bfloat16),
        compiler_params=params(),
    )(points, returned)


def tally_cells(ids, cells):
    fine = 64
    high = (ids[None, :] // fine == jnp.arange(cells // fine, dtype=jnp.int32)[:, None]).astype(jnp.bfloat16)
    low = (ids[None, :] % fine == jnp.arange(fine, dtype=jnp.int32)[:, None]).astype(jnp.bfloat16)
    return lax.dot_general(high, low, (((1,), (1,)), ((), ())), preferred_element_type=jnp.float32).reshape(cells)


def on_device(points, point_cell, conv_weight, conv_bias, neighbors):
    width = points.shape[0]
    owners = lax.axis_size("space")
    groups = lax.axis_size("chan")
    cap = points.shape[2] // owners
    blocks = neighbors.shape[0]
    share = blocks // groups
    flat = points.reshape(width, owners * cap)
    ids = point_cell[0]
    weight_all = lax.all_gather(conv_weight, "chan", axis=0)
    counts = tally_cells(ids, blocks * CELLS)
    active = jnp.where(counts > 0.0, 1.0, 0.0).astype(jnp.float32)
    arrived = lax.all_to_all(split_slots(flat, owners, cap), "space", split_axis=0, concat_axis=0, tiled=True)
    own = pool(arrived, ids, counts, groups)
    left = lax.ppermute(own, "space", [(i, i + 1) for i in range(owners - 1)])
    right = lax.ppermute(own, "space", [(i + 1, i) for i in range(owners - 1)])
    margins = build_margins(neighbors, left, own, right, conv_bias.reshape(1, width), groups, share)
    spread = lax.all_to_all(margins, "chan", split_axis=0, concat_axis=0, tiled=True)
    mine = lax.dynamic_slice_in_dim(active, lax.axis_index("chan") * (share * CELLS), share * CELLS, 0)
    finished = convolve(spread, weight_all, mine.reshape(1, share * CELLS), share)
    finished = finished.reshape(groups, width, share * CELLS)
    parts = lax.all_to_all(finished, "chan", split_axis=0, concat_axis=0, tiled=True)
    picked, voxel_out = pick(parts, ids, owners, cap)
    returned = lax.all_to_all(picked, "space", split_axis=0, concat_axis=0, tiled=True)
    point_out = add_back(flat, returned).reshape(points.shape)
    return (voxel_out, point_out)


def solution(mesh):
    return jax.shard_map(
        on_device,
        mesh=mesh,
        in_specs=(
            P("chan", "space", None),
            P("space", None),
            P(None, "chan", None),
            P("chan"),
            P("space", None),
        ),
        out_specs=(P("chan", "space"), P("chan", "space", None)),
        check_vma=False,
    )
```

time: 665 us -> 199 us (0.30)
  the two profiles are of different devices: /device:TPU:11 before, /device:TPU:0 now
where the time goes in v1:
time: 199 us
  waiting for transfers between devices  63.3 us (32%)
  blocking collectives  51 us (26%)
  Pallas kernels  50.6 us (25%)
  between operations  14.1 us (7%)
  starting transfers between devices  12.9 us (6%)
  local copies, waits for them, and re-layouts  4.87 us (2%)
    all_to_all x1, waiting for transfers between devices, on_device(): lax.all_to_all(margins, 'chan', split_axis=0, concat_axis=0, tiled=True)  36.5 us
    all_to_all x1, blocking collectives, on_device(): lax.all_to_all(picked, 'space', split_axis=0, concat_axis=0, tiled=True)  30.9 us
    all_to_all x1, waiting for transfers between devices, on_device(): lax.all_to_all(split_slots(flat, owners, cap), 'space', split_axis=0, con...  22.7 us
    all_to_all x1, blocking collectives, on_device(): lax.all_to_all(finished, 'chan', split_axis=0, concat_axis=0, tiled=True)  20.1 us
    pallas_call x1, Pallas kernels, pick(): pl.pallas_call(functools.partial(pick_kernel, groups), grid=(owners,), in...  13.8 us
    pallas_call x1, Pallas kernels, pool(): pl.pallas_call(functools.partial(pool_kernel, groups, low_cells), grid=(o...  13.1 us
    pallas_call x1, Pallas kernels, convolve(): pl.pallas_call(functools.partial(conv_kernel, share), in_specs=[vmem] * 3...  7.36 us
    pallas_call x1, Pallas kernels, add_back(): pl.pallas_call(add_kernel, grid=(owners,), in_specs=[pl.BlockSpec((width,...  6.17 us
  transfers between devices with their start and end apart: 5, of which 4 were waited for; matrix products, arithmetic and copies ran while one was open for 2% of the time, Pallas kernels for 9%

profile of v1, /device:TPU:0, one launch (start us, length us, event | category | flops | bytes accessed | tf_op | source)
XLA Modules:
  0.0 198.7 jit_solution(3052095186652944446)
XLA Ops:
  7.2 5.6 %shard_map.68 = bf16[8,64,2048]{2,1,0:T(8,128)(2,1)} custom-call(bf16[64,16384]{1,0:T(8,128)(2,1)} %bitcast.12), custom_call_target="tpu_custom_call" | custom-call | tf_op jit(solution)/shard_map/pallas_call | solution.py:25
  12.8 0.0 copy-start.2
  12.8 5.3 %all-to-all-start = ((bf16[8,64,2048]{2,1,0:T(8,128)(2,1)}), bf16[8,64,2048]{2,1,0:T(8,128)(2,1)S(1)}, u32[]{:S(2)}, u32[]{:S(2)}) async-start(bf16[8,64,2048]{2,1,0:T(8,128)(2,1)} %shard_map.68), calls=%async_computation | async-start | bytes 4194304 | tf_op jit(solution)/shard_map/all_to_all | solution.py:270
  18.1 0.0 all-gather.3.cloned.1.call-start
  18.2 0.7 all-gather.3.cloned.1.call-update
  18.9 0.0 copy-done.2
  18.9 0.3 and_select_fusion.1
  19.2 0.5 iota_compare_fusion.2.clone.5
  19.7 0.1 and_select_fusion
  19.8 1.1 compare_select_fusion.3
  21.0 0.1 reshape_reshape.3
  21.1 1.0 copy.8
  22.1 22.7 %all-to-all-done.x_ref = bf16[8,64,2048]{2,1,0:T(8,128)(2,1)S(1)} async-done(((bf16[8,64,2048]{2,1,0:T(8,128)(2,1)}), bf16[8,64,2048]{2,1,0:T(8,128)(2,1)S(1)}, u32[]{:S(2)}, u32[]{:S(2)}) %all-to-all-start) | async-done | bytes 2097184 | tf_op jit(solution)/shard_map/all_to_all | solution.py:270
  44.7 0.0 copy-start
  44.7 1.3 copy-done
  46.1 13.1 %shard_map.69.own_ref = bf16[1024,256]{1,0:T(8,128)(2,1)} custom-call(bf16[8,64,2048]{2,1,0:T(8,128)(2,1)} %copy-done, s32[8,1,2048]{2,1,0:T(1,128)} %bitcast.19, f32[1024,4]{1,0:T(8,128)} %bitcast.16), custom_call_target="tpu_custom_call" | custom-call | tf_op jit(solution)/shard_map/pallas_call | solution.py:69
  59.2 1.3 collective-permute-start
  60.5 1.3 collective-permute-start.1
  61.8 0.4 collective-permute-done.left_ref
  62.2 0.0 copy-start.3
  62.2 3.0 %collective-permute-done.1.right_ref = bf16[1024,256]{1,0:T(8,128)(2,1)S(1)} collective-permute-done((bf16[1024,256]{1,0:T(8,128)(2,1)}, bf16[1024,256]{1,0:T(8,128)(2,1)S(1)}, u32[]{:S(2)}, u32[]{:S(2)}) %collective-permute-start.1) | collective-permute-done | bytes 524320 | tf_op jit(solution)/shard_map/ppermute | solution.py:273
  65.2 0.0 copy-start.4
  65.2 0.0 copy-done.3
  65.2 0.8 copy-done.4
  66.1 4.5 %shard_map.70 = bf16[4,1008,128]{2,1,0:T(8,128)(2,1)} custom-call(s32[8,27]{1,0:T(8,128)} %nb_ref.1, bf16[1024,256]{1,0:T(8,128)(2,1)} %copy-done.3, bf16[1024,256]{1,0:T(8,128)(2,1)} %shard_map.69.own_ref, bf16[1024,256]{1,0:T(8,128)(2,1)} %copy-done.4, bf16[1,64]{1,0:T(2,128)(2,1)} %bitcast.24), custom_call_target="tpu_custom_call" | custom-call | tf_op jit(solution)/shard_map/pallas_call | solution.py:123
  70.5 4.9 %all-to-all-start.1 = ((bf16[4,1008,128]{2,1,0:T(8,128)(2,1)}), bf16[4,1008,128]{2,1,0:T(8,128)(2,1)S(1)}, u32[]{:S(2)}, u32[]{:S(2)}) async-start(bf16[4,1008,128]{2,1,0:T(8,128)(2,1)} %shard_map.70), calls=%async_computation.1 | async-start | bytes 2064384 | tf_op jit(solution)/shard_map/all_to_all | solution.py:275
  75.4 0.1 select_n.25
  75.5 0.6 dynamic_slice.3
  76.1 36.5 %all-to-all-done.1.m_ref = bf16[4,1008,128]{2,1,0:T(8,128)(2,1)S(1)} async-done(((bf16[4,1008,128]{2,1,0:T(8,128)(2,1)}), bf16[4,1008,128]{2,1,0:T(8,128)(2,1)S(1)}, u32[]{:S(2)}, u32[]{:S(2)}) %all-to-all-start.1) | async-done | bytes 1032224 | tf_op jit(solution)/shard_map/all_to_all | solution.py:275
  112.6 0.0 copy-start.1
  112.6 0.0 all-gather.3.cloned.1.call-done
  112.6 1.0 copy-done.1
  113.6 7.4 %shard_map.71 = bf16[256,1024]{1,0:T(8,128)(2,1)} custom-call(bf16[4,1008,128]{2,1,0:T(8,128)(2,1)} %copy-done.1, bf16[4,27,64,256]{3,2,1,0:T(8,128)(2,1)} %bitcast.14, f32[1,1024]{1,0:T(1,128)} %bitcast.23), custom_call_target="tpu_custom_call" | custom-call | tf_op jit(solution)/shard_map/pallas_call | solution.py:177
  121.0 20.1 %all_to_all.20 = bf16[4,64,1024]{2,1,0:T(8,128)(2,1)} all-to-all(bf16[4,64,1024]{2,1,0:T(8,128)(2,1)} %bitcast.17), channel_id=1, replica_groups=mesh['space'=8,'chan'=4] {'chan'}, dimensions={0} | all-to-all | bytes 1048576 | tf_op jit(solution)/shard_map/all_to_all | solution.py:279
  141.0 13.8 %shard_map.72 = (bf16[8,64,2048]{2,1,0:T(8,128)(2,1)}, bf16[64,4096]{1,0:T(8,128)(2,1)}) custom-call(bf16[256,1024]{1,0:T(8,128)(2,1)} %bitcast.18, s32[8,1,2048]{2,1,0:T(1,128)} %bitcast.20), custom_call_target="tpu_custom_call" | custom-call | tf_op jit(solution)/shard_map/pallas_call | solution.py:213
  154.8 30.9 %all_to_all.21.r_ref = bf16[8,64,2048]{2,1,0:T(8,128)(2,1)} all-to-all(bf16[8,64,2048]{2,1,0:T(8,128)(2,1)} %get-tuple-element.5), channel_id=1, replica_groups=mesh['space'=8,'chan'=4] {'space'}, dimensions={0} | all-to-all | bytes 4194304 | tf_op jit(solution)/shard_map/all_to_all | solution.py:281
  185.7 6.2 %shard_map.73 = bf16[64,16384]{1,0:T(8,128)(2,1)} custom-call(bf16[64,16384]{1,0:T(8,128)(2,1)} %bitcast.13, bf16[8,64,2048]{2,1,0:T(8,128)(2,1)} %all_to_all.21.r_ref), custom_call_target="tpu_custom_call" | custom-call | tf_op jit(solution)/shard_map/pallas_call | solution.py:238
Async XLA Ops:
  12.8 6.1 %copy-start.2 = (s32[1,16384]{1,0:T(1,128)S(1)}, s32[1,16384]{1,0:T(1,128)}, u32[]{:S(2)}) copy-start(s32[1,16384]{1,0:T(1,128)} %param.6) | copy-start | bytes 196612
  12.8 31.9 %all-to-all-start = ((bf16[8,64,2048]{2,1,0:T(8,128)(2,1)}), bf16[8,64,2048]{2,1,0:T(8,128)(2,1)S(1)}, u32[]{:S(2)}, u32[]{:S(2)}) async-start(bf16[8,64,2048]{2,1,0:T(8,128)(2,1)} %shard_map.68), calls=%async_computation | async-start | bytes 4194304 | tf_op jit(solution)/shard_map/all_to_all | solution.py:270
  18.1 94.5 %all-gather.3.cloned.1.call-start = ((), (), s32[]{:S(2)}) async-start(), calls=%async_computation.4 | async-start | bytes 4423680 | tf_op jit(solution)/shard_map/all_gather | solution.py:267
  44.7 1.3 copy-start
  59.2 3.0 %collective-permute-start = (bf16[1024,256]{1,0:T(8,128)(2,1)}, bf16[1024,256]{1,0:T(8,128)(2,1)S(1)}, u32[]{:S(2)}, u32[]{:S(2)}) collective-permute-start(bf16[1024,256]{1,0:T(8,128)(2,1)} %shard_map.69.own_ref), channel_id=1, source_target_pairs={{0,4},{4,8},{8,12},{12,16},{16,20},{20,24},{24,28},{1,5},{5,9},{9,... | collective-permute-start | bytes 1572872 | tf_op jit(solution)/shard_map/ppermute | solution.py:272
  60.5 4.7 %collective-permute-start.1 = (bf16[1024,256]{1,0:T(8,128)(2,1)}, bf16[1024,256]{1,0:T(8,128)(2,1)S(1)}, u32[]{:S(2)}, u32[]{:S(2)}) collective-permute-start(bf16[1024,256]{1,0:T(8,128)(2,1)} %shard_map.69.own_ref), channel_id=1, source_target_pairs={{4,0},{8,4},{12,8},{16,12},{20,16},{24,20},{28,24},{5,1},{9,5},{13... | collective-permute-start | bytes 1572872 | tf_op jit(solution)/shard_map/ppermute | solution.py:273
  62.2 3.0 %copy-start.3 = (bf16[1024,256]{1,0:T(8,128)(2,1)}, bf16[1024,256]{1,0:T(8,128)(2,1)S(1)}, u32[]{:S(2)}) copy-start(bf16[1024,256]{1,0:T(8,128)(2,1)S(1)} %collective-permute-done.left_ref) | copy-start | bytes 1572868
  65.2 0.8 copy-start.4
  70.5 42.1 %all-to-all-start.1 = ((bf16[4,1008,128]{2,1,0:T(8,128)(2,1)}), bf16[4,1008,128]{2,1,0:T(8,128)(2,1)S(1)}, u32[]{:S(2)}, u32[]{:S(2)}) async-start(bf16[4,1008,128]{2,1,0:T(8,128)(2,1)} %shard_map.70), calls=%async_computation.1 | async-start | bytes 2064384 | tf_op jit(solution)/shard_map/all_to_all | solution.py:275
  112.6 1.0 copy-start.1
Sparse Core Ops, SparseCore 0:
  20.5 85.2 all-gather.2

commit v2 on v1

--- a/solution.py
+++ b/solution.py
@@ -9,6 +9,7 @@
 
 VMEM_LIMIT = 60 * 1024 * 1024
 CELLS = 512
+MESH = pl.DeviceIdType.MESH
 ROWS = 1008
 
 
@@ -16,69 +17,148 @@
     return pltpu.CompilerParams(vmem_limit_bytes=VMEM_LIMIT)
 
 
-def split_kernel(x_ref, o_ref):
-    o_ref[0] = x_ref[...]
-
-
-def split_slots(points, owners, cap):
+def greet(axis, count):
+    me = lax.axis_index(axis)
+    barrier = pltpu.get_barrier_semaphore()
+
+    def signal(t, carry):
+        pl.semaphore_signal(barrier, inc=1, device_id={axis: lax.rem(me + t, count)}, device_id_type=MESH)
+        return carry
+
+    lax.fori_loop(1, count, signal, 0)
+    pl.semaphore_wait(barrier, count - 1)
+    return me
+
+
+def remote_params(collective_id):
+    return pltpu.CompilerParams(
+        vmem_limit_bytes=VMEM_LIMIT, collective_id=collective_id, has_side_effects=True
+    )
+
+
+def pool_kernel(groups, low_cells, owners, x_ref, id_ref, count_ref, o_ref, held, acc_ref, send_sem, recv_sem, own_sem):
+    width, rows = held.shape[1], held.shape[2]
+    me = greet("space", owners)
+
+    def chunk(d):
+        return x_ref.at[:, pl.ds(pl.multiple_of(d * rows, rows), rows)]
+
+    def copy(t):
+        peer = lax.rem(me + t, owners)
+        return pltpu.make_async_remote_copy(
+            src_ref=chunk(peer),
+            dst_ref=held.at[t],
+            send_sem=send_sem.at[t],
+            recv_sem=recv_sem.at[t],
+            device_id={"space": peer},
+            device_id_type=MESH,
+        )
+
+    def send(t, carry):
+        copy(t).start()
+        return carry
+
+    lax.fori_loop(1, owners, send, 0)
+    own = pltpu.make_async_copy(chunk(me), held.at[0], own_sem)
+    own.start()
+    acc_ref[...] = jnp.zeros_like(acc_ref)
+    spots = lax.broadcasted_iota(jnp.int32, (low_cells, rows), 0)
+
+    def add_chunk(t):
+        ids = id_ref[lax.rem(me + owners - t, owners)]
+        high = ids // low_cells
+        low = ids % low_cells
+        x = held[t]
+        zero = jnp.zeros_like(x)
+        masked = jnp.concatenate(
+            [jnp.where(jnp.broadcast_to(high, x.shape) == g, x, zero) for g in range(groups)], axis=0
+        )
+        onehot = jnp.where(spots == low, 1.0, 0.0).astype(jnp.bfloat16)
+        acc_ref[...] += lax.dot_general(
+            onehot, masked, (((1,), (1,)), ((), ())), preferred_element_type=jnp.float32
+        )
+
+    own.wait()
+    add_chunk(0)
+
+    def take(t, carry):
+        copy(t).wait_recv()
+        add_chunk(t)
+        return carry
+
+    lax.fori_loop(1, owners, take, 0)
+    for g in range(groups):
+        lanes = slice(g * width, (g + 1) * width)
+        tally = jnp.maximum(count_ref[:, g : g + 1], 1.0)
+        o_ref[:, lanes] = (acc_ref[:, lanes] / tally).astype(jnp.bfloat16)
+
+    def close(t, carry):
+        copy(t).wait_send()
+        return carry
+
+    lax.fori_loop(1, owners, close, 0)
+
+
+def pool(points, ids, counts, groups, owners, cap):
     width = points.shape[0]
-    return pl.pallas_call(
-        split_kernel,
-        grid=(owners,),
-        in_specs=[pl.BlockSpec((width, cap), lambda d: (0, d))],
-        out_specs=pl.BlockSpec((1, width, cap), lambda d: (d, 0, 0)),
-        out_shape=jax.ShapeDtypeStruct((owners, width, cap), jnp.bfloat16),
-        compiler_params=params(),
-    )(points)
-
-
-def pool_kernel(groups, low_cells, x_ref, id_ref, count_ref, o_ref, acc_ref):
-    turn = pl.program_id(0)
-    width, rows = x_ref.shape[1], x_ref.shape[2]
-
-    @pl.when(turn == 0)
-    def _():
-        acc_ref[...] = jnp.zeros_like(acc_ref)
-
-    ids = id_ref[0]
-    high = ids // low_cells
-    low = ids % low_cells
-    x = x_ref[0]
-    zero = jnp.zeros_like(x)
-    masked = jnp.concatenate(
-        [jnp.where(jnp.broadcast_to(high, x.shape) == g, x, zero) for g in range(groups)], axis=0
-    )
-    spots = lax.broadcasted_iota(jnp.int32, (low_cells, rows), 0)
-    onehot = jnp.where(spots == low, 1.0, 0.0).astype(jnp.bfloat16)
-    acc_ref[...] += lax.dot_general(
-        onehot, masked, (((1,), (1,)), ((), ())), preferred_element_type=jnp.float32
-    )
-
-    @pl.when(turn == pl.num_programs(0) - 1)
-    def _():
-        for g in range(groups):
-            lanes = slice(g * width, (g + 1) * width)
-            tally = jnp.maximum(count_ref[:, g : g + 1], 1.0)
-            o_ref[:, lanes] = (acc_ref[:, lanes] / tally).astype(jnp.bfloat16)
-
-
-def pool(arrived, ids, counts, groups):
-    owners, width, cap = arrived.shape
     low_cells = counts.shape[0] // groups
     by_group = counts.reshape(groups, low_cells).T
-    return pl.pallas_call(
-        functools.partial(pool_kernel, groups, low_cells),
-        grid=(owners,),
-        in_specs=[
-            pl.BlockSpec((1, width, cap), lambda s: (s, 0, 0)),
-            pl.BlockSpec((1, 1, cap), lambda s: (s, 0, 0)),
-            pl.BlockSpec((low_cells, groups), lambda s: (0, 0)),
+    vmem = pl.BlockSpec(memory_space=pltpu.VMEM)
+    return pl.pallas_call(
+        functools.partial(pool_kernel, groups, low_cells, owners),
+        in_specs=[pl.BlockSpec(memory_space=pl.ANY), vmem, vmem],
+        out_specs=vmem,
+        out_shape=jax.ShapeDtypeStruct((low_cells, groups * width), jnp.bfloat16),
+        scratch_shapes=[
+            pltpu.VMEM((owners, width, cap), jnp.bfloat16),
+            pltpu.VMEM((low_cells, groups * width), jnp.float32),
+            pltpu.SemaphoreType.DMA((owners,)),
+            pltpu.SemaphoreType.DMA((owners,)),
+            pltpu.SemaphoreType.DMA,
         ],
-        out_specs=pl.BlockSpec((low_cells, groups * width), lambda s: (0, 0)),
-        out_shape=jax.ShapeDtypeStruct((low_cells, groups * width), jnp.bfloat16),
-        scratch_shapes=[pltpu.VMEM((low_cells, groups * width), jnp.float32)],
-        compiler_params=params(),
-    )(arrived, ids.reshape(owners, 1, cap), by_group)
+        compiler_params=remote_params(0),
+    )(points, ids.reshape(owners, 1, cap), by_group)
+
+
+def exchange_kernel(axis, count, x_ref, o_ref, send_sem, recv_sem):
+    me = greet(axis, count)
+
+    def copy(t, landing):
+        peer = lax.rem(me + t, count)
+        return pltpu.make_async_remote_copy(
+            src_ref=x_ref.at[peer],
+            dst_ref=o_ref.at[landing],
+            send_sem=send_sem.at[t],
+            recv_sem=recv_sem.at[t],
+            device_id={axis: peer},
+            device_id_type=MESH,
+        )
+
+    def send(t, carry):
+        copy(t, me).start()
+        return carry
+
+    def close(t, carry):
+        copy(t, lax.rem(me + count - t, count)).wait_recv()
+        copy(t, me).wait_send()
+        return carry
+
+    lax.fori_loop(1, count, send, 0)
+    o_ref[me] = x_ref[me]
+    lax.fori_loop(1, count, close, 0)
+
+
+def exchange(x, axis, collective_id):
+    count = lax.axis_size(axis)
+    vmem = pl.BlockSpec(memory_space=pltpu.VMEM)
+    return pl.pallas_call(
+        functools.partial(exchange_kernel, axis, count),
+        in_specs=[vmem],
+        out_specs=vmem,
+        out_shape=jax.ShapeDtypeStruct(x.shape, x.dtype),
+        scratch_shapes=[pltpu.SemaphoreType.DMA((count,)), pltpu.SemaphoreType.DMA((count,))],
+        compiler_params=remote_params(collective_id),
+    )(x)
 
 
 def margin_kernel(groups, share, nb_ref, left_ref, own_ref, right_ref, bias_ref, o_ref, v_ref, m_ref):
@@ -187,65 +267,73 @@
     )(spread, weight_all, active)
 
 
-def pick_kernel(groups, v_ref, id_ref, o_ref, vox_ref):
+def return_kernel(groups, owners, v_ref, id_ref, p_ref, o_ref, found_ref, held, send_sem, recv_sem):
     width, low_cells = v_ref.shape[0] // groups, v_ref.shape[1]
     rows = id_ref.shape[2]
-
-    @pl.when(pl.program_id(0) == 0)
-    def _():
+    me = greet("space", owners)
+    spots = lax.broadcasted_iota(jnp.int32, (low_cells, rows), 0)
+
+    def copy(t):
+        return pltpu.make_async_remote_copy(
+            src_ref=found_ref.at[t],
+            dst_ref=held.at[t],
+            send_sem=send_sem.at[t],
+            recv_sem=recv_sem.at[t],
+            device_id={"space": lax.rem(me + t, owners)},
+            device_id_type=MESH,
+        )
+
+    def pick(s):
+        ids = id_ref[s]
+        high = ids // low_cells
+        low = ids % low_cells
+        onehot = jnp.where(spots == low, 1.0, 0.0).astype(jnp.bfloat16)
+        found = jnp.dot(v_ref[...], onehot, preferred_element_type=jnp.float32)
+        total = jnp.zeros((width, rows), jnp.float32)
         for g in range(groups):
-            vox_ref[:, g * low_cells : (g + 1) * low_cells] = v_ref[g * width : (g + 1) * width, :]
-
-    ids = id_ref[0]
-    high = ids // low_cells
-    low = ids % low_cells
-    spots = lax.broadcasted_iota(jnp.int32, (low_cells, rows), 0)
-    onehot = jnp.where(spots == low, 1.0, 0.0).astype(jnp.bfloat16)
-    found = jnp.dot(v_ref[...], onehot, preferred_element_type=jnp.float32)
-    total = jnp.zeros((width, rows), jnp.float32)
-    for g in range(groups):
-        total = jnp.where(jnp.broadcast_to(high, total.shape) == g, found[g * width : (g + 1) * width], total)
-    o_ref[0] = total.astype(jnp.bfloat16)
-
-
-def pick(parts, ids, owners, cap):
+            total = jnp.where(jnp.broadcast_to(high, total.shape) == g, found[g * width : (g + 1) * width], total)
+        return total
+
+    def add(d, values):
+        at = pl.ds(pl.multiple_of(d * rows, rows), rows)
+        o_ref[:, at] = (p_ref[:, at].astype(jnp.float32) + values).astype(jnp.bfloat16)
+
+    def send(t, carry):
+        found_ref[t] = pick(lax.rem(me + t, owners)).astype(jnp.bfloat16)
+        copy(t).start()
+        return carry
+
+    def take(t, carry):
+        copy(t).wait_recv()
+        add(lax.rem(me + owners - t, owners), held[t].astype(jnp.float32))
+        return carry
+
+    def close(t, carry):
+        copy(t).wait_send()
+        return carry
+
+    lax.fori_loop(1, owners, send, 0)
+    add(me, pick(me))
+    lax.fori_loop(1, owners, take, 0)
+    lax.fori_loop(1, owners, close, 0)
+
+
+def give_back(parts, ids, points, owners, cap):
     groups, width, low_cells = parts.shape
-    return pl.pallas_call(
-        functools.partial(pick_kernel, groups),
-        grid=(owners,),
-        in_specs=[
-            pl.BlockSpec((groups * width, low_cells), lambda s: (0, 0)),
-            pl.BlockSpec((1, 1, cap), lambda s: (s, 0, 0)),
+    vmem = pl.BlockSpec(memory_space=pltpu.VMEM)
+    return pl.pallas_call(
+        functools.partial(return_kernel, groups, owners),
+        in_specs=[vmem] * 3,
+        out_specs=vmem,
+        out_shape=jax.ShapeDtypeStruct(points.shape, jnp.bfloat16),
+        scratch_shapes=[
+            pltpu.VMEM((owners, width, cap), jnp.bfloat16),
+            pltpu.VMEM((owners, width, cap), jnp.bfloat16),
+            pltpu.SemaphoreType.DMA((owners,)),
+            pltpu.SemaphoreType.DMA((owners,)),
         ],
-        out_specs=[
-            pl.BlockSpec((1, width, cap), lambda s: (s, 0, 0)),
-            pl.BlockSpec((width, groups * low_cells), lambda s: (0, 0)),
-        ],
-        out_shape=[
-            jax.ShapeDtypeStruct((owners, width, cap), jnp.bfloat16),
-            jax.ShapeDtypeStruct((width, groups * low_cells), jnp.bfloat16),
-        ],
-        compiler_params=params(),
-    )(parts.reshape(groups * width, low_cells), ids.reshape(owners, 1, cap))
-
-
-def add_kernel(p_ref, r_ref, o_ref):
-    o_ref[...] = (p_ref[...].astype(jnp.float32) + r_ref[0].astype(jnp.float32)).astype(jnp.bfloat16)
-
-
-def add_back(points, returned):
-    owners, width, cap = returned.shape
-    return pl.pallas_call(
-        add_kernel,
-        grid=(owners,),
-        in_specs=[
-            pl.BlockSpec((width, cap), lambda d: (0, d)),
-            pl.BlockSpec((1, width, cap), lambda d: (d, 0, 0)),
-        ],
-        out_specs=pl.BlockSpec((width, cap), lambda d: (0, d)),
-        out_shape=jax.ShapeDtypeStruct(points.shape, jnp.bfloat16),
-        compiler_params=params(),
-    )(points, returned)
+        compiler_params=remote_params(3),
+    )(parts.reshape(groups * width, low_cells), ids.reshape(owners, 1, cap), points)
 
 
 def tally_cells(ids, cells):
@@ -267,19 +355,17 @@
     weight_all = lax.all_gather(conv_weight, "chan", axis=0)
     counts = tally_cells(ids, blocks * CELLS)
     active = jnp.where(counts > 0.0, 1.0, 0.0).astype(jnp.float32)
-    arrived = lax.all_to_all(split_slots(flat, owners, cap), "space", split_axis=0, concat_axis=0, tiled=True)
-    own = pool(arrived, ids, counts, groups)
+    own = pool(flat, ids, counts, groups, owners, cap)
     left = lax.ppermute(own, "space", [(i, i + 1) for i in range(owners - 1)])
     right = lax.ppermute(own, "space", [(i + 1, i) for i in range(owners - 1)])
     margins = build_margins(neighbors, left, own, right, conv_bias.reshape(1, width), groups, share)
-    spread = lax.all_to_all(margins, "chan", split_axis=0, concat_axis=0, tiled=True)
+    spread = exchange(margins, "chan", 1)
     mine = lax.dynamic_slice_in_dim(active, lax.axis_index("chan") * (share * CELLS), share * CELLS, 0)
     finished = convolve(spread, weight_all, mine.reshape(1, share * CELLS), share)
     finished = finished.reshape(groups, width, share * CELLS)
-    parts = lax.all_to_all(finished, "chan", split_axis=0, concat_axis=0, tiled=True)
-    picked, voxel_out = pick(parts, ids, owners, cap)
-    returned = lax.all_to_all(picked, "space", split_axis=0, concat_axis=0, tiled=True)
-    point_out = add_back(flat, returned).reshape(points.shape)
+    parts = exchange(finished, "chan", 2)
+    voxel_out = jnp.transpose(parts, (1, 0, 2)).reshape(width, blocks * CELLS)
+    point_out = give_back(parts, ids, flat, owners, cap).reshape(points.shape)
     return (voxel_out, point_out)
 
 

time: 199 us -> 170 us (0.85)
  the two profiles are of different devices: /device:TPU:0 before, /device:TPU:11 now
where the time goes in v2:
time: 170 us
  Pallas kernels  127 us (75%)
  waiting for transfers between devices  14.5 us (9%)
  between operations  14.1 us (8%)
  local copies, waits for them, and re-layouts  6.45 us (4%)
  starting transfers between devices  4.54 us (3%)
  other arithmetic  1.77 us (1%)
    pallas_call x2, Pallas kernels, exchange(): pl.pallas_call(functools.partial(exchange_kernel, axis, count), in_specs=...  49.8 us
    pallas_call x1, Pallas kernels, give_back(): pl.pallas_call(functools.partial(return_kernel, groups, owners), in_specs...  34.1 us
    pallas_call x1, Pallas kernels, pool(): pl.pallas_call(functools.partial(pool_kernel, groups, low_cells, owners),...  31.7 us
    ppermute x1, waiting for transfers between devices, on_device(): right = lax.ppermute(own, 'space', [(i + 1, i) for i in range(owners - 1)])  10.5 us
    pallas_call x1, Pallas kernels, convolve(): pl.pallas_call(functools.partial(conv_kernel, share), in_specs=[vmem] * 3...  7.37 us
    pallas_call x1, Pallas kernels, build_margins(): pl.pallas_call(functools.partial(margin_kernel, groups, share), in_specs=...  4.48 us
    unnamed x7, local copies, waits for them, and re-layouts  3.84 us
  transfers between devices with their start and end apart: 3, of which 2 were waited for; matrix products, arithmetic and copies ran while one was open for 3% of the time, Pallas kernels for 42%

profile of v2, /device:TPU:11, one launch (start us, length us, event | category | flops | bytes accessed | tf_op | source)
XLA Modules:
  0.0 170.0 jit_solution(17544300919275889929)
XLA Ops:
  7.2 0.0 all-gather.3.cloned.1.call-start
  7.2 0.7 all-gather.3.cloned.1.call-update
  7.9 1.1 and_select_fusion.1
  9.0 0.1 and_select_fusion
  9.1 0.5 iota_compare_fusion.2.clone.5
  9.7 1.1 compare_select_fusion.3
  10.8 0.1 reshape_reshape.3
  10.9 1.0 copy.9
  11.9 31.7 %shard_map.68.own_ref = bf16[1024,256]{1,0:T(8,128)(2,1)} custom-call(bf16[64,16384]{1,0:T(8,128)(2,1)} %bitcast.15, s32[8,1,2048]{2,1,0:T(1,128)} %bitcast.23, f32[1024,4]{1,0:T(8,128)} %bitcast.22), custom_call_target="tpu_custom_call" | custom-call | tf_op jit(solution)/shard_map/pallas_call | solution.py:107
  43.7 2.1 %collective-permute-start = (bf16[1024,256]{1,0:T(8,128)(2,1)}, bf16[1024,256]{1,0:T(8,128)(2,1)S(1)}, u32[]{:S(2)}, u32[]{:S(2)}) collective-permute-start(bf16[1024,256]{1,0:T(8,128)(2,1)} %shard_map.68.own_ref), channel_id=1, source_target_pairs={{0,4},{4,8},{8,12},{12,16},{16,20},{20,24},{24,28},{1,5},{5,9},{9,... | collective-permute-start | bytes 1572872 | tf_op jit(solution)/shard_map/ppermute | solution.py:359
  45.7 2.5 %collective-permute-start.1 = (bf16[1024,256]{1,0:T(8,128)(2,1)}, bf16[1024,256]{1,0:T(8,128)(2,1)S(1)}, u32[]{:S(2)}, u32[]{:S(2)}) collective-permute-start(bf16[1024,256]{1,0:T(8,128)(2,1)} %shard_map.68.own_ref), channel_id=1, source_target_pairs={{4,0},{8,4},{12,8},{16,12},{20,16},{24,20},{28,24},{5,1},{9,5},{13... | collective-permute-start | bytes 1572872 | tf_op jit(solution)/shard_map/ppermute | solution.py:360
  48.2 0.1 select_n.25
  48.3 0.6 dynamic_slice.3
  48.9 3.3 %collective-permute-done.left_ref = bf16[1024,256]{1,0:T(8,128)(2,1)S(1)} collective-permute-done((bf16[1024,256]{1,0:T(8,128)(2,1)}, bf16[1024,256]{1,0:T(8,128)(2,1)S(1)}, u32[]{:S(2)}, u32[]{:S(2)}) %collective-permute-start) | collective-permute-done | bytes 524320 | tf_op jit(solution)/shard_map/ppermute | solution.py:359
  52.1 0.0 copy-start.1
  52.1 10.5 %collective-permute-done.1.right_ref = bf16[1024,256]{1,0:T(8,128)(2,1)S(1)} collective-permute-done((bf16[1024,256]{1,0:T(8,128)(2,1)}, bf16[1024,256]{1,0:T(8,128)(2,1)S(1)}, u32[]{:S(2)}, u32[]{:S(2)}) %collective-permute-start.1) | collective-permute-done | bytes 524320 | tf_op jit(solution)/shard_map/ppermute | solution.py:360
  62.7 0.0 copy-start.2
  62.7 0.0 copy-done.1
  62.7 0.8 copy-done.2
  63.5 4.5 %shard_map.69.x_ref = bf16[4,1008,128]{2,1,0:T(8,128)(2,1)} custom-call(s32[8,27]{1,0:T(8,128)} %nb_ref.1, bf16[1024,256]{1,0:T(8,128)(2,1)} %copy-done.1, bf16[1024,256]{1,0:T(8,128)(2,1)} %shard_map.68.own_ref, bf16[1024,256]{1,0:T(8,128)(2,1)} %copy-done.2, bf16[1,64]{1,0:T(2,128)(2,1)} %bitcast.29), custom_call_target="tpu_custom_call" | custom-call | tf_op jit(solution)/shard_map/pallas_call | solution.py:203
  67.9 34.6 %shard_map.70.m_ref = bf16[4,1008,128]{2,1,0:T(8,128)(2,1)} custom-call(bf16[4,1008,128]{2,1,0:T(8,128)(2,1)} %shard_map.69.x_ref), custom_call_target="tpu_custom_call" | custom-call | tf_op jit(solution)/shard_map/pallas_call | solution.py:154
  102.6 0.0 all-gather.3.cloned.1.call-done
  102.6 7.4 %shard_map.71 = bf16[256,1024]{1,0:T(8,128)(2,1)} custom-call(bf16[4,1008,128]{2,1,0:T(8,128)(2,1)} %shard_map.70.m_ref, bf16[4,27,64,256]{3,2,1,0:T(8,128)(2,1)} %bitcast.20, f32[1,1024]{1,0:T(1,128)} %bitcast.28), custom_call_target="tpu_custom_call" | custom-call | tf_op jit(solution)/shard_map/pallas_call | solution.py:257
  110.0 15.2 %shard_map.72 = bf16[4,64,1024]{2,1,0:T(8,128)(2,1)} custom-call(bf16[4,64,1024]{2,1,0:T(8,128)(2,1)} %bitcast.21), custom_call_target="tpu_custom_call" | custom-call | tf_op jit(solution)/shard_map/pallas_call | solution.py:154
  125.2 0.0 copy-start
  125.2 34.1 %shard_map.73 = bf16[64,16384]{1,0:T(8,128)(2,1)} custom-call(bf16[256,1024]{1,0:T(8,128)(2,1)} %bitcast.18, s32[8,1,2048]{2,1,0:T(1,128)} %bitcast.24, bf16[64,16384]{1,0:T(8,128)(2,1)} %bitcast.16), custom_call_target="tpu_custom_call" | custom-call | tf_op jit(solution)/shard_map/pallas_call | solution.py:324
  159.2 0.0 copy-done
  159.3 0.8 copy.11
  160.1 3.0 %copy.15 = bf16[64,1,16384]{2,0,1:T(8,128)(2,1)} copy(bf16[64,1,16384]{2,0,1:T(8,128)(2,1)} %bitcast.17) | data formatting | bytes 4194304
Async XLA Ops:
  7.2 95.4 %all-gather.3.cloned.1.call-start = ((), (), s32[]{:S(2)}) async-start(), calls=%async_computation | async-start | bytes 4423680 | tf_op jit(solution)/shard_map/all_gather | solution.py:355
  43.7 8.5 %collective-permute-start = (bf16[1024,256]{1,0:T(8,128)(2,1)}, bf16[1024,256]{1,0:T(8,128)(2,1)S(1)}, u32[]{:S(2)}, u32[]{:S(2)}) collective-permute-start(bf16[1024,256]{1,0:T(8,128)(2,1)} %shard_map.68.own_ref), channel_id=1, source_target_pairs={{0,4},{4,8},{8,12},{12,16},{16,20},{20,24},{24,28},{1,5},{5,9},{9,... | collective-permute-start | bytes 1572872 | tf_op jit(solution)/shard_map/ppermute | solution.py:359
  45.7 16.9 %collective-permute-start.1 = (bf16[1024,256]{1,0:T(8,128)(2,1)}, bf16[1024,256]{1,0:T(8,128)(2,1)S(1)}, u32[]{:S(2)}, u32[]{:S(2)}) collective-permute-start(bf16[1024,256]{1,0:T(8,128)(2,1)} %shard_map.68.own_ref), channel_id=1, source_target_pairs={{4,0},{8,4},{12,8},{16,12},{20,16},{24,20},{28,24},{5,1},{9,5},{13... | collective-permute-start | bytes 1572872 | tf_op jit(solution)/shard_map/ppermute | solution.py:360
  52.1 10.5 %copy-start.1 = (bf16[1024,256]{1,0:T(8,128)(2,1)}, bf16[1024,256]{1,0:T(8,128)(2,1)S(1)}, u32[]{:S(2)}) copy-start(bf16[1024,256]{1,0:T(8,128)(2,1)S(1)} %collective-permute-done.left_ref) | copy-start | bytes 1572868
  62.7 0.8 copy-start.2
  125.2 34.1 %copy-start = (bf16[4,64,1024]{2,1,0:T(8,128)(2,1)S(1)}, bf16[4,64,1024]{2,1,0:T(8,128)(2,1)}, u32[]{:S(2)}) copy-start(bf16[4,64,1024]{2,1,0:T(8,128)(2,1)} %shard_map.72) | copy-start | bytes 1572868
Sparse Core Ops, SparseCore 0:
  9.5 74.9 all-gather.2

commit v3 on v2

--- a/solution.py
+++ b/solution.py
@@ -214,7 +214,8 @@
 
 
 def conv_kernel(share, m_ref, w_ref, act_ref, o_ref, f_ref, q_ref):
-    groups, _, width, outs = w_ref.shape
+    halves, groups, _, part, outs = w_ref.shape
+    width = halves * part
     wide = groups * width
     for lb in range(share):
         for g in range(groups):
@@ -237,7 +238,8 @@
                 for j in range(3):
                     windows.append(q_ref[k, lb, i : i + 4, j : j + 8].reshape(CELLS, wide))
                     for g in range(groups):
-                        weights.append(w_ref[g, 9 * i + 3 * j + k])
+                        for half in range(halves):
+                            weights.append(w_ref[half, g, 9 * i + 3 * j + k])
             term = jnp.dot(
                 jnp.concatenate(windows, axis=1),
                 jnp.concatenate(weights, axis=0),
@@ -252,7 +254,7 @@
 
 
 def convolve(spread, weight_all, active, share):
-    groups, _, width, outs = weight_all.shape
+    halves, groups, _, part, outs = weight_all.shape
     vmem = pl.BlockSpec(memory_space=pltpu.VMEM)
     return pl.pallas_call(
         functools.partial(conv_kernel, share),
@@ -260,8 +262,8 @@
         out_specs=vmem,
         out_shape=jax.ShapeDtypeStruct((outs, share * CELLS), jnp.bfloat16),
         scratch_shapes=[
-            pltpu.VMEM((share, ROWS, groups * width), jnp.float32),
-            pltpu.VMEM((3, share, 6, 10, 16, groups * width), jnp.bfloat16),
+            pltpu.VMEM((share, ROWS, groups * halves * part), jnp.float32),
+            pltpu.VMEM((3, share, 6, 10, 16, groups * halves * part), jnp.bfloat16),
         ],
         compiler_params=params(),
     )(spread, weight_all, active)
@@ -343,6 +345,17 @@
     return lax.dot_general(high, low, (((1,), (1,)), ((), ())), preferred_element_type=jnp.float32).reshape(cells)
 
 
+def gather_half(conv_weight):
+    half = conv_weight.shape[1] // 2
+    mine = lax.dynamic_slice_in_dim(conv_weight, lax.rem(lax.axis_index("space"), 2) * half, half, 1)
+    return lax.all_gather(mine, "chan", axis=0)
+
+
+def swap_halves(gathered, owners):
+    pairs = [[i, i + 1] for i in range(0, owners, 2)]
+    return lax.all_gather(gathered, "space", axis=0, axis_index_groups=pairs)
+
+
 def on_device(points, point_cell, conv_weight, conv_bias, neighbors):
     width = points.shape[0]
     owners = lax.axis_size("space")
@@ -352,10 +365,12 @@
     share = blocks // groups
     flat = points.reshape(width, owners * cap)
     ids = point_cell[0]
-    weight_all = lax.all_gather(conv_weight, "chan", axis=0)
+    gathered = gather_half(conv_weight)
     counts = tally_cells(ids, blocks * CELLS)
     active = jnp.where(counts > 0.0, 1.0, 0.0).astype(jnp.float32)
     own = pool(flat, ids, counts, groups, owners, cap)
+    gathered, own = lax.optimization_barrier((gathered, own))
+    weight_all = swap_halves(gathered, owners)
     left = lax.ppermute(own, "space", [(i, i + 1) for i in range(owners - 1)])
     right = lax.ppermute(own, "space", [(i + 1, i) for i in range(owners - 1)])
     margins = build_margins(neighbors, left, own, right, conv_bias.reshape(1, width), groups, share)

time: 170 us -> 167 us (0.982)
  Pallas kernels: 127 us -> 120 us
  local copies, waits for them, and re-layouts: 6.45 us -> 9.4 us
  starting transfers between devices: 4.54 us -> 6.72 us
    pallas_call x2, Pallas kernels: 49.8 us -> 42.6 us  [exchange(): pl.pallas_call(functools.partial(exchange_kernel, axis, count), in_specs=...]
    all_gather x1 -> x2, waiting for transfers between devices: 0.02 us -> 5 us  [the longest x1 4.98 us: gather_half(): return lax.all_gather(mine, 'chan', axis=0)]
    ppermute x1, waiting for transfers between devices: 10.5 us -> 7.44 us  [on_device(): right = lax.ppermute(own, 'space', [(i + 1, i) for i in range(owners - 1)])]
    ppermute x1, waiting for transfers between devices: 3.29 us -> 0.55 us  [on_device(): left = lax.ppermute(own, 'space', [(i, i + 1) for i in range(owners - 1)])]
  transfers between devices with their start and end apart: 3 -> 4, of which waited for: 2 -> 3; matrix products, arithmetic and copies ran while one was open for 3% -> 3% of each run, Pallas kernels for 42% -> 38%
where the time goes in v3:
time: 167 us
  Pallas kernels  120 us (72%)
  between operations  14.1 us (8%)
  waiting for transfers between devices  13 us (8%)
  local copies, waits for them, and re-layouts  9.4 us (6%)
  starting transfers between devices  6.72 us (4%)
  other arithmetic  1.77 us (1%)
    pallas_call x2, Pallas kernels, exchange(): pl.pallas_call(functools.partial(exchange_kernel, axis, count), in_specs=...  42.6 us
    pallas_call x1, Pallas kernels, give_back(): pl.pallas_call(functools.partial(return_kernel, groups, owners), in_specs...  34.1 us
    pallas_call x1, Pallas kernels, pool(): pl.pallas_call(functools.partial(pool_kernel, groups, low_cells, owners),...  31.7 us
    ppermute x1, waiting for transfers between devices, on_device(): right = lax.ppermute(own, 'space', [(i + 1, i) for i in range(owners - 1)])  7.44 us
    pallas_call x1, Pallas kernels, convolve(): pl.pallas_call(functools.partial(conv_kernel, share), in_specs=[vmem] * 3...  7.37 us
    all_gather x1, waiting for transfers between devices, gather_half(): return lax.all_gather(mine, 'chan', axis=0)  4.98 us
    unnamed x7, local copies, waits for them, and re-layouts  4.95 us
    pallas_call x1, Pallas kernels, build_margins(): pl.pallas_call(functools.partial(margin_kernel, groups, share), in_specs=...  4.48 us
  transfers between devices with their start and end apart: 4, of which 3 were waited for; matrix products, arithmetic and copies ran while one was open for 3% of the time, Pallas kernels for 38%

profile of v3, /device:TPU:11, one launch (start us, length us, event | category | flops | bytes accessed | tf_op | source)
XLA Modules:
  0.0 166.5 jit_solution(15668171787920335030)
XLA Ops:
  7.2 0.0 copy-start
  7.2 0.0 all-gather.5.cloned.1.call-start
  7.2 1.1 copy-done
  8.3 0.8 constant_dynamic-slice_fusion
  9.1 0.0 all-gather.5.cloned.1.call-update
  9.2 0.0 all-gather.7.cloned.1.call-start
  9.2 1.1 and_select_fusion.1
  10.4 0.5 iota_compare_fusion.2.clone.5
  10.9 0.1 and_select_fusion
  11.0 1.1 compare_select_fusion.3
  12.1 0.1 reshape_reshape.3
  12.2 1.0 copy.9
  13.3 31.7 %shard_map.68.own_ref = bf16[1024,256]{1,0:T(8,128)(2,1)} custom-call(bf16[64,16384]{1,0:T(8,128)(2,1)} %bitcast.16, s32[8,1,2048]{2,1,0:T(1,128)} %bitcast.25, f32[1024,4]{1,0:T(8,128)} %bitcast.23), custom_call_target="tpu_custom_call" | custom-call | tf_op jit(solution)/shard_map/pallas_call | solution.py:107
  45.0 5.0 %all-gather.5.cloned.1.call-done = bf16[108,32,256]{2,1,0:T(8,128)(2,1)} async-done(((bf16[27,32,256]{2,1,0:T(8,128)(2,1)}), bf16[108,32,256]{2,1,0:T(8,128)(2,1)}) %all-gather.5.cloned.1.call-update) | async-done | bytes 1769488 | tf_op jit(solution)/shard_map/all_gather | solution.py:351
  50.0 0.0 all-gather.7.cloned.1.call-update
  50.0 3.1 %collective-permute-start.1 = (bf16[1024,256]{1,0:T(8,128)(2,1)}, bf16[1024,256]{1,0:T(8,128)(2,1)S(1)}, u32[]{:S(2)}, u32[]{:S(2)}) collective-permute-start(bf16[1024,256]{1,0:T(8,128)(2,1)} %shard_map.68.own_ref), channel_id=1, source_target_pairs={{4,0},{8,4},{12,8},{16,12},{20,16},{24,20},{28,24},{5,1},{9,5},{13... | collective-permute-start | bytes 1572872 | tf_op jit(solution)/shard_map/ppermute | solution.py:375
  53.1 3.6 %collective-permute-start = (bf16[1024,256]{1,0:T(8,128)(2,1)}, bf16[1024,256]{1,0:T(8,128)(2,1)S(1)}, u32[]{:S(2)}, u32[]{:S(2)}) collective-permute-start(bf16[1024,256]{1,0:T(8,128)(2,1)} %shard_map.68.own_ref), channel_id=1, source_target_pairs={{0,4},{4,8},{8,12},{12,16},{16,20},{20,24},{24,28},{1,5},{5,9},{9,... | collective-permute-start | bytes 1572872 | tf_op jit(solution)/shard_map/ppermute | solution.py:374
  56.7 0.1 select_n.29
  56.7 0.6 dynamic_slice.7
  57.3 7.4 %collective-permute-done.1.right_ref = bf16[1024,256]{1,0:T(8,128)(2,1)S(1)} collective-permute-done((bf16[1024,256]{1,0:T(8,128)(2,1)}, bf16[1024,256]{1,0:T(8,128)(2,1)S(1)}, u32[]{:S(2)}, u32[]{:S(2)}) %collective-permute-start.1) | collective-permute-done | bytes 524320 | tf_op jit(solution)/shard_map/ppermute | solution.py:375
  64.8 0.0 copy-start.1
  64.8 0.6 collective-permute-done.left_ref
  65.3 0.0 copy-start.2
  65.3 0.3 copy-done.1
  65.6 0.5 copy-done.2
  66.1 4.5 %shard_map.69.x_ref = bf16[4,1008,128]{2,1,0:T(8,128)(2,1)} custom-call(s32[8,27]{1,0:T(8,128)} %nb_ref.1, bf16[1024,256]{1,0:T(8,128)(2,1)} %copy-done.2, bf16[1024,256]{1,0:T(8,128)(2,1)} %shard_map.68.own_ref, bf16[1024,256]{1,0:T(8,128)(2,1)} %copy-done.1, bf16[1,64]{1,0:T(2,128)(2,1)} %bitcast.31), custom_call_target="tpu_custom_call" | custom-call | tf_op jit(solution)/shard_map/pallas_call | solution.py:203
  70.6 26.9 %shard_map.70.m_ref = bf16[4,1008,128]{2,1,0:T(8,128)(2,1)} custom-call(bf16[4,1008,128]{2,1,0:T(8,128)(2,1)} %shard_map.69.x_ref), custom_call_target="tpu_custom_call" | custom-call | tf_op jit(solution)/shard_map/pallas_call | solution.py:154
  97.5 0.0 all-gather.7.cloned.1.call-done
  97.5 7.4 %shard_map.71 = bf16[256,1024]{1,0:T(8,128)(2,1)} custom-call(bf16[4,1008,128]{2,1,0:T(8,128)(2,1)} %shard_map.70.m_ref, bf16[2,4,27,32,256]{4,3,2,1,0:T(8,128)(2,1)} %bitcast.21, f32[1,1024]{1,0:T(1,128)} %bitcast.30), custom_call_target="tpu_custom_call" | custom-call | tf_op jit(solution)/shard_map/pallas_call | solution.py:259
  104.9 15.8 %shard_map.72 = bf16[4,64,1024]{2,1,0:T(8,128)(2,1)} custom-call(bf16[4,64,1024]{2,1,0:T(8,128)(2,1)} %bitcast.22), custom_call_target="tpu_custom_call" | custom-call | tf_op jit(solution)/shard_map/pallas_call | solution.py:154
  120.7 1.9 %copy.11 = bf16[4,8,8,1024]{3,2,0,1:T(8,128)(2,1)} copy(bf16[4,8,8,1024]{3,2,1,0:T(8,128)(2,1)} %bitcast.19) | data formatting | bytes 1048576 | tf_op jit(solution)/shard_map/reshape | solution.py:382
  122.5 34.1 %shard_map.73 = bf16[64,16384]{1,0:T(8,128)(2,1)} custom-call(bf16[256,1024]{1,0:T(8,128)(2,1)} %bitcast.20, s32[8,1,2048]{2,1,0:T(1,128)} %bitcast.26, bf16[64,16384]{1,0:T(8,128)(2,1)} %bitcast.17), custom_call_target="tpu_custom_call" | custom-call | tf_op jit(solution)/shard_map/pallas_call | solution.py:326
  156.6 3.0 %copy.15 = bf16[64,1,16384]{2,0,1:T(8,128)(2,1)} copy(bf16[64,1,16384]{2,0,1:T(8,128)(2,1)} %bitcast.18) | data formatting | bytes 4194304
Async XLA Ops:
  7.2 1.2 copy-start
  7.2 42.8 %all-gather.5.cloned.1.call-start = ((), (), s32[]{:S(2)}) async-start(), calls=%async_computation | async-start | bytes 2211840 | tf_op jit(solution)/shard_map/all_gather | solution.py:351
  9.2 88.4 %all-gather.7.cloned.1.call-start = ((), (), s32[]{:S(2)}) async-start(), calls=%async_computation.1 | async-start | bytes 5308416 | tf_op jit(solution)/shard_map/all_gather | solution.py:356
  50.0 14.8 %collective-permute-start.1 = (bf16[1024,256]{1,0:T(8,128)(2,1)}, bf16[1024,256]{1,0:T(8,128)(2,1)S(1)}, u32[]{:S(2)}, u32[]{:S(2)}) collective-permute-start(bf16[1024,256]{1,0:T(8,128)(2,1)} %shard_map.68.own_ref), channel_id=1, source_target_pairs={{4,0},{8,4},{12,8},{16,12},{20,16},{24,20},{28,24},{5,1},{9,5},{13... | collective-permute-start | bytes 1572872 | tf_op jit(solution)/shard_map/ppermute | solution.py:375
  53.1 12.2 %collective-permute-start = (bf16[1024,256]{1,0:T(8,128)(2,1)}, bf16[1024,256]{1,0:T(8,128)(2,1)S(1)}, u32[]{:S(2)}, u32[]{:S(2)}) collective-permute-start(bf16[1024,256]{1,0:T(8,128)(2,1)} %shard_map.68.own_ref), channel_id=1, source_target_pairs={{0,4},{4,8},{8,12},{12,16},{16,20},{20,24},{24,28},{1,5},{5,9},{9,... | collective-permute-start | bytes 1572872 | tf_op jit(solution)/shard_map/ppermute | solution.py:374
  64.8 0.8 copy-start.1
  65.3 0.8 copy-start.2
Sparse Core Ops, SparseCore 0:
  10.1 39.8 all-gather.4
  51.5 13.8 all-gather.6

commit v4 on v3

--- a/solution.py
+++ b/solution.py
@@ -369,11 +369,11 @@
     counts = tally_cells(ids, blocks * CELLS)
     active = jnp.where(counts > 0.0, 1.0, 0.0).astype(jnp.float32)
     own = pool(flat, ids, counts, groups, owners, cap)
-    gathered, own = lax.optimization_barrier((gathered, own))
-    weight_all = swap_halves(gathered, owners)
     left = lax.ppermute(own, "space", [(i, i + 1) for i in range(owners - 1)])
     right = lax.ppermute(own, "space", [(i + 1, i) for i in range(owners - 1)])
     margins = build_margins(neighbors, left, own, right, conv_bias.reshape(1, width), groups, share)
+    gathered, margins = lax.optimization_barrier((gathered, margins))
+    weight_all = swap_halves(gathered, owners)
     spread = exchange(margins, "chan", 1)
     mine = lax.dynamic_slice_in_dim(active, lax.axis_index("chan") * (share * CELLS), share * CELLS, 0)
     finished = convolve(spread, weight_all, mine.reshape(1, share * CELLS), share)

time: 167 us -> 166 us (level)
    ppermute x1, waiting for transfers between devices: 0.55 us -> 6.15 us  [on_device(): left = lax.ppermute(own, 'space', [(i, i + 1) for i in range(owners - 1)])]
    all_gather x1, waiting for transfers between devices: 4.98 us -> 0.01 us  [gather_half(): return lax.all_gather(mine, 'chan', axis=0)]
    ppermute x1, waiting for transfers between devices: 7.44 us -> 5.31 us  [on_device(): right = lax.ppermute(own, 'space', [(i + 1, i) for i in range(owners - 1)])]
    pallas_call x2, Pallas kernels: 42.6 us -> 44.4 us  [exchange(): pl.pallas_call(functools.partial(exchange_kernel, axis, count), in_specs=...]
  transfers between devices with their start and end apart: 4 -> 4, of which waited for: 3 -> 2; matrix products, arithmetic and copies ran while one was open for 3% -> 3% of each run, Pallas kernels for 38% -> 39%
where the time goes in v4:
time: 166 us
  Pallas kernels  121 us (73%)
  between operations  14.1 us (8%)
  waiting for transfers between devices  11.5 us (7%)
  local copies, waits for them, and re-layouts  9.42 us (6%)
  starting transfers between devices  6.72 us (4%)
  other arithmetic  1.77 us (1%)
    pallas_call x2, Pallas kernels, exchange(): pl.pallas_call(functools.partial(exchange_kernel, axis, count), in_specs=...  44.4 us
    pallas_call x1, Pallas kernels, give_back(): pl.pallas_call(functools.partial(return_kernel, groups, owners), in_specs...  33.4 us
    pallas_call x1, Pallas kernels, pool(): pl.pallas_call(functools.partial(pool_kernel, groups, low_cells, owners),...  31.5 us
    pallas_call x1, Pallas kernels, convolve(): pl.pallas_call(functools.partial(conv_kernel, share), in_specs=[vmem] * 3...  7.37 us
    ppermute x1, waiting for transfers between devices, on_device(): left = lax.ppermute(own, 'space', [(i, i + 1) for i in range(owners - 1)])  6.15 us
    ppermute x1, waiting for transfers between devices, on_device(): right = lax.ppermute(own, 'space', [(i + 1, i) for i in range(owners - 1)])  5.31 us
    unnamed x7, local copies, waits for them, and re-layouts  4.95 us
    ppermute x1, starting transfers between devices, on_device(): left = lax.ppermute(own, 'space', [(i, i + 1) for i in range(owners - 1)])  4.72 us
  transfers between devices with their start and end apart: 4, of which 2 were waited for; matrix products, arithmetic and copies ran while one was open for 3% of the time, Pallas kernels for 39%

profile of v4, /device:TPU:11, one launch (start us, length us, event | category | flops | bytes accessed | tf_op | source)
XLA Modules:
  0.0 165.8 jit_solution(9351739586763930605)
XLA Ops:
  7.2 0.0 copy-start
  7.2 0.0 all-gather.5.cloned.1.call-start
  7.2 1.1 copy-done
  8.3 0.8 constant_dynamic-slice_fusion
  9.2 0.0 all-gather.5.cloned.1.call-update
  9.2 0.0 all-gather.7.cloned.1.call-start
  9.2 1.1 and_select_fusion.1
  10.4 0.5 iota_compare_fusion.2.clone.5
  10.9 0.1 and_select_fusion
  11.0 1.1 compare_select_fusion.3
  12.2 0.1 reshape_reshape.3
  12.2 1.0 copy.9
  13.3 31.5 %shard_map.68.own_ref = bf16[1024,256]{1,0:T(8,128)(2,1)} custom-call(bf16[64,16384]{1,0:T(8,128)(2,1)} %bitcast.16, s32[8,1,2048]{2,1,0:T(1,128)} %bitcast.25, f32[1024,4]{1,0:T(8,128)} %bitcast.23), custom_call_target="tpu_custom_call" | custom-call | tf_op jit(solution)/shard_map/pallas_call | solution.py:107
  44.8 1.9 %collective-permute-start.1 = (bf16[1024,256]{1,0:T(8,128)(2,1)}, bf16[1024,256]{1,0:T(8,128)(2,1)S(1)}, u32[]{:S(2)}, u32[]{:S(2)}) collective-permute-start(bf16[1024,256]{1,0:T(8,128)(2,1)} %shard_map.68.own_ref), channel_id=1, source_target_pairs={{4,0},{8,4},{12,8},{16,12},{20,16},{24,20},{28,24},{5,1},{9,5},{13... | collective-permute-start | bytes 1572872 | tf_op jit(solution)/shard_map/ppermute | solution.py:373
  46.7 4.7 %collective-permute-start = (bf16[1024,256]{1,0:T(8,128)(2,1)}, bf16[1024,256]{1,0:T(8,128)(2,1)S(1)}, u32[]{:S(2)}, u32[]{:S(2)}) collective-permute-start(bf16[1024,256]{1,0:T(8,128)(2,1)} %shard_map.68.own_ref), channel_id=1, source_target_pairs={{0,4},{4,8},{8,12},{12,16},{16,20},{20,24},{24,28},{1,5},{5,9},{9,... | collective-permute-start | bytes 1572872 | tf_op jit(solution)/shard_map/ppermute | solution.py:372
  51.4 5.3 %collective-permute-done.1.right_ref = bf16[1024,256]{1,0:T(8,128)(2,1)S(1)} collective-permute-done((bf16[1024,256]{1,0:T(8,128)(2,1)}, bf16[1024,256]{1,0:T(8,128)(2,1)S(1)}, u32[]{:S(2)}, u32[]{:S(2)}) %collective-permute-start.1) | collective-permute-done | bytes 524320 | tf_op jit(solution)/shard_map/ppermute | solution.py:373
  56.7 0.0 copy-start.1
  56.7 6.2 %collective-permute-done.left_ref = bf16[1024,256]{1,0:T(8,128)(2,1)S(1)} collective-permute-done((bf16[1024,256]{1,0:T(8,128)(2,1)}, bf16[1024,256]{1,0:T(8,128)(2,1)S(1)}, u32[]{:S(2)}, u32[]{:S(2)}) %collective-permute-start) | collective-permute-done | bytes 524320 | tf_op jit(solution)/shard_map/ppermute | solution.py:372
  62.9 0.0 copy-start.2
  62.9 0.0 copy-done.1
  62.9 0.8 copy-done.2
  63.7 4.5 %shard_map.69.x_ref = bf16[4,1008,128]{2,1,0:T(8,128)(2,1)} custom-call(s32[8,27]{1,0:T(8,128)} %nb_ref.1, bf16[1024,256]{1,0:T(8,128)(2,1)} %copy-done.2, bf16[1024,256]{1,0:T(8,128)(2,1)} %shard_map.68.own_ref, bf16[1024,256]{1,0:T(8,128)(2,1)} %copy-done.1, bf16[1,64]{1,0:T(2,128)(2,1)} %bitcast.31), custom_call_target="tpu_custom_call" | custom-call | tf_op jit(solution)/shard_map/pallas_call | solution.py:203
  68.2 0.0 all-gather.5.cloned.1.call-done
  68.2 0.0 all-gather.7.cloned.1.call-update
  68.2 0.1 select_n.29
  68.3 0.6 dynamic_slice.7
  68.9 28.0 %shard_map.70.m_ref = bf16[4,1008,128]{2,1,0:T(8,128)(2,1)} custom-call(bf16[4,1008,128]{2,1,0:T(8,128)(2,1)} %shard_map.69.x_ref), custom_call_target="tpu_custom_call" | custom-call | tf_op jit(solution)/shard_map/pallas_call | solution.py:154
  96.9 0.0 all-gather.7.cloned.1.call-done
  96.9 7.4 %shard_map.71 = bf16[256,1024]{1,0:T(8,128)(2,1)} custom-call(bf16[4,1008,128]{2,1,0:T(8,128)(2,1)} %shard_map.70.m_ref, bf16[2,4,27,32,256]{4,3,2,1,0:T(8,128)(2,1)} %bitcast.21, f32[1,1024]{1,0:T(1,128)} %bitcast.30), custom_call_target="tpu_custom_call" | custom-call | tf_op jit(solution)/shard_map/pallas_call | solution.py:259
  104.3 16.3 %shard_map.72 = bf16[4,64,1024]{2,1,0:T(8,128)(2,1)} custom-call(bf16[4,64,1024]{2,1,0:T(8,128)(2,1)} %bitcast.22), custom_call_target="tpu_custom_call" | custom-call | tf_op jit(solution)/shard_map/pallas_call | solution.py:154
  120.6 1.9 %copy.11 = bf16[4,8,8,1024]{3,2,0,1:T(8,128)(2,1)} copy(bf16[4,8,8,1024]{3,2,1,0:T(8,128)(2,1)} %bitcast.19) | data formatting | bytes 1048576 | tf_op jit(solution)/shard_map/reshape | solution.py:382
  122.5 33.4 %shard_map.73 = bf16[64,16384]{1,0:T(8,128)(2,1)} custom-call(bf16[256,1024]{1,0:T(8,128)(2,1)} %bitcast.20, s32[8,1,2048]{2,1,0:T(1,128)} %bitcast.26, bf16[64,16384]{1,0:T(8,128)(2,1)} %bitcast.17), custom_call_target="tpu_custom_call" | custom-call | tf_op jit(solution)/shard_map/pallas_call | solution.py:326
  155.9 3.0 %copy.15 = bf16[64,1,16384]{2,0,1:T(8,128)(2,1)} copy(bf16[64,1,16384]{2,0,1:T(8,128)(2,1)} %bitcast.18) | data formatting | bytes 4194304
Async XLA Ops:
  7.2 1.2 copy-start
  7.2 61.0 %all-gather.5.cloned.1.call-start = ((), (), s32[]{:S(2)}) async-start(), calls=%async_computation | async-start | bytes 2211840 | tf_op jit(solution)/shard_map/all_gather | solution.py:351
  9.2 87.7 %all-gather.7.cloned.1.call-start = ((), (), s32[]{:S(2)}) async-start(), calls=%async_computation.1 | async-start | bytes 5308416 | tf_op jit(solution)/shard_map/all_gather | solution.py:356
  44.8 12.0 %collective-permute-start.1 = (bf16[1024,256]{1,0:T(8,128)(2,1)}, bf16[1024,256]{1,0:T(8,128)(2,1)S(1)}, u32[]{:S(2)}, u32[]{:S(2)}) collective-permute-start(bf16[1024,256]{1,0:T(8,128)(2,1)} %shard_map.68.own_ref), channel_id=1, source_target_pairs={{4,0},{8,4},{12,8},{16,12},{20,16},{24,20},{28,24},{5,1},{9,5},{13... | collective-permute-start | bytes 1572872 | tf_op jit(solution)/shard_map/ppermute | solution.py:373
  46.7 16.2 %collective-permute-start = (bf16[1024,256]{1,0:T(8,128)(2,1)}, bf16[1024,256]{1,0:T(8,128)(2,1)S(1)}, u32[]{:S(2)}, u32[]{:S(2)}) collective-permute-start(bf16[1024,256]{1,0:T(8,128)(2,1)} %shard_map.68.own_ref), channel_id=1, source_target_pairs={{0,4},{4,8},{8,12},{12,16},{16,20},{20,24},{24,28},{1,5},{5,9},{9,... | collective-permute-start | bytes 1572872 | tf_op jit(solution)/shard_map/ppermute | solution.py:372
  56.7 6.2 %copy-start.1 = (bf16[1024,256]{1,0:T(8,128)(2,1)}, bf16[1024,256]{1,0:T(8,128)(2,1)S(1)}, u32[]{:S(2)}) copy-start(bf16[1024,256]{1,0:T(8,128)(2,1)S(1)} %collective-permute-done.1.right_ref) | copy-start | bytes 1572868
  62.9 0.8 copy-start.2
Sparse Core Ops, SparseCore 0:
  9.6 39.8 all-gather.4
  68.3 15.1 all-gather.6
